TPU v7x, 32 devices: a whole 2x2x4 slice. The times are simulated.
32 devices in a mesh: parts: 2 (over y), mp: 4 (over z), dp: 4 (over x, core).
Axes of the slice: x: 2, y: 2, z: 4, core: 2. Of those that a mesh axis runs over, the one named last changes fastest.
Arguments:
- embeddings: bfloat16 [2048, 1024], P(('parts', 'dp')), parts along dimension 0, may hold values from -16 to 16
- w_in: bfloat16 [1024, 8192], P(None, 'mp'), may hold values from -0.1875 to 0.1875
- w_out: bfloat16 [8192, 1024], P('mp'), may hold values from -0.0625 to 0.0625
- means: bfloat16 [8192, 1024], P('mp'), may hold values from -2.09375 to 2.09375
- precisions: bfloat16 [8192, 1024], P('mp'), may hold values from 0.04 to 0.16
- log_weight: float32 [8192], P('mp'), may hold values from -4 to 0
Outputs:
- counts: float32 [16384], P(('parts', 'mp')), parts along dimension 0
- first_moment: float32 [2048, 8192], P(('parts', 'dp'), 'mp'), parts along dimension 0
- second_moment: float32 [2048, 8192], P(('parts', 'dp'), 'mp'), parts along dimension 0
- grad_w_in: bfloat16 [2048, 8192], P(('parts', 'dp'), 'mp'), parts along dimension 0
- grad_w_out_t: bfloat16 [2048, 8192], P(('parts', 'dp'), 'mp'), parts along dimension 0
- grad_embed: bfloat16 [2048, 1024], P(('parts', 'dp')), parts along dimension 0
There are 2 independent parts, one for each index of `parts`. A program takes and returns all parts, laid end to end along the dimension named above; an argument that names none is the same for every part. Nothing has to cross between parts.
All inputs are finite; a program needn't handle non-finite values.
Results may differ from a plain program's by a relative error of at most 0.028.
Values may be sent and summed in bfloat16 or wider, within the bound.
A program may use at most 128 MiB of HBM per device.

v0:
```python
import jax
import jax.numpy as jnp
from jax import lax
from jax.sharding import PartitionSpec as P


def combined_all(part, axis, combine):
    gathered = jax.tree.map(lambda a: lax.all_gather(a, axis), part)

    def take(source):
        return jax.tree.map(lambda a: lax.dynamic_index_in_dim(a, source, 0, False), gathered)

    return lax.fori_loop(
        1, lax.axis_size(axis), lambda source, state: combine(state, take(source)), take(0)
    )


def combine_rows(first, second):
    top = jnp.maximum(first[0], second[0])
    total = first[1] * jnp.exp(first[0] - top) + second[1] * jnp.exp(second[0] - top)
    return (top, total)


def body(embeddings, w_in, w_out, means, precisions, log_weight):
    contract_rows = (((0,), (0,)), ((), ()))
    contract_cols = (((1,), (1,)), ((), ()))
    pre = jnp.dot(embeddings, w_in, preferred_element_type=jnp.float32)
    hidden = jax.nn.silu(pre).astype(jnp.bfloat16)
    partial_value = jnp.dot(hidden, w_out, preferred_element_type=jnp.float32)
    head = lax.psum(partial_value, "mp").astype(jnp.bfloat16)
    head_f = head.astype(jnp.float32)
    squares = (head_f * head_f).astype(jnp.bfloat16)
    means_f = means.astype(jnp.float32)
    prec_f = precisions.astype(jnp.float32)
    weighted = (means_f * prec_f).astype(jnp.bfloat16)
    offset = (
        log_weight
        + 0.5 * jnp.sum(jnp.log(prec_f), axis=1)
        - 0.5 * jnp.sum(means_f * means_f * prec_f, axis=1)
    )
    scores = offset[None, :] + lax.dot_general(
        head, weighted, contract_cols, preferred_element_type=jnp.float32
    )
    scores = scores - 0.5 * lax.dot_general(
        squares, precisions, contract_cols, preferred_element_type=jnp.float32
    )
    local_top = jnp.max(scores, axis=1)
    local_total = jnp.sum(jnp.exp(scores - local_top[:, None]), axis=1)
    top, total = combined_all((local_top, local_total), "mp", combine_rows)
    lse = top + jnp.log(total)
    resp = jnp.exp(scores - lse[:, None])
    resp_b = resp.astype(jnp.bfloat16)
    counts = lax.psum(jnp.sum(resp, axis=0), "dp")
    local_comp = resp_b.shape[1]
    first = lax.dot_general(head, resp_b, contract_rows, preferred_element_type=jnp.float32)
    second = lax.dot_general(squares, resp_b, contract_rows, preferred_element_type=jnp.float32)
    moments = lax.psum_scatter(
        jnp.concatenate([first, second], axis=1).astype(jnp.bfloat16),
        "dp",
        scatter_dimension=0,
        tiled=True,
    ).astype(jnp.float32)
    first_moment = moments[:, :local_comp]
    second_moment = moments[:, local_comp:]
    along = jnp.dot(resp_b, precisions, preferred_element_type=jnp.float32)
    shifted = jnp.dot(resp_b, weighted, preferred_element_type=jnp.float32)
    grad_term = head_f * along - shifted
    grad_head = lax.psum(grad_term.astype(jnp.bfloat16), "mp")
    back = lax.dot_general(grad_head, w_out, contract_cols, preferred_element_type=jnp.float32)
    sigma = jax.nn.sigmoid(pre)
    grad_pre = (back * sigma * (1.0 + pre * (1.0 - sigma))).astype(jnp.bfloat16)
    embed_term = lax.dot_general(grad_pre, w_in, contract_cols, preferred_element_type=jnp.float32)
    grad_embed = lax.psum(embed_term.astype(jnp.bfloat16), "mp")
    local_hidden = hidden.shape[1]
    term_in = lax.dot_general(
        embeddings, grad_pre, contract_rows, preferred_element_type=jnp.float32
    )
    term_out = lax.dot_general(grad_head, hidden, contract_rows, preferred_element_type=jnp.float32)
    weight_sums = lax.psum_scatter(
        jnp.concatenate([term_in, term_out], axis=1).astype(jnp.bfloat16),
        "dp",
        scatter_dimension=0,
        tiled=True,
    ).astype(jnp.float32)
    grad_w_in = weight_sums[:, :local_hidden].astype(jnp.bfloat16)
    grad_w_out_t = weight_sums[:, local_hidden:].astype(jnp.bfloat16)
    return (counts, first_moment, second_moment, grad_w_in, grad_w_out_t, grad_embed)


def solution(mesh):
    return jax.shard_map(
        body,
        mesh=mesh,
        in_specs=(
            P(("parts", "dp"), None),
            P(None, "mp"),
            P("mp", None),
            P("mp", None),
            P("mp", None),
            P("mp"),
        ),
        out_specs=(
            P(("parts", "mp")),
            P(("parts", "dp"), "mp"),
            P(("parts", "dp"), "mp"),
            P(("parts", "dp"), "mp"),
            P(("parts", "dp"), "mp"),
            P(("parts", "dp"), None),
        ),
        check_vma=False,
    )
```

profile of v0, /device:TPU:1, one launch (start us, length us, event | category | flops | bytes accessed | tf_op | source)
XLA Modules:
  0.0 268.1 jit_solution(3075487471116822724)
XLA Ops:
  8.0 0.0 copy-start
  8.0 0.0 all-reduce.4.cloned.1.call-start
  8.1 1.0 copy-done
  9.0 0.0 copy-start.8
  9.0 3.6 %fusion.24 = f32[256,2048]{1,0:T(8,128)S(1)} fusion(bf16[256,1024]{1,0:T(8,128)(2,1)S(1)} %copy-done, bf16[1024,2048]{1,0:T(8,128)(2,1)} %param.9), kind=kOutput, calls=%fused_computation.43 | convolution fusion | flops 1073741824 | bytes 6815744 | tf_op jit(solution)/shard_map/dot_general | solution.py:27
  12.6 0.0 copy-start.10
  12.7 1.3 copy-done.10
  14.0 0.0 copy-done.8
  14.0 1.3 fusion.20
  15.3 40.6 %all-reduce.7 = bf16[256,1024]{1,0:T(8,128)(2,1)S(1)} all-reduce(f32[256,1024]{1,0:T(8,128)S(1)} %fusion.20), channel_id=1, replica_groups=mesh['parts'=2,'mp'=4,'dp'=4] {'mp'}, use_global_device_ids=true, to_apply=%region_2.3 | all-reduce | flops 262144 | bytes 1572864 | tf_op jit(solution)/shard_map/psum | solution.py:30
  55.9 0.0 copy-start.1
  56.0 5.2 %fusion = (f32[2048]{0:T(1024)S(1)}, f32[2048]{0:T(1024)S(1)}) fusion(bf16[2048,1024]{1,0:T(8,128)(2,1)} %param.12, bf16[2048,1024]{1,0:T(8,128)(2,1)} %param.11), kind=kLoop, calls=%fused_computation.7 | loop fusion | flops 12578816 | bytes 8404992 | tf_op jit(solution)/shard_map/reduce_sum | solution.py:38
  61.2 0.0 copy-done.1
  61.2 0.0 copy-start.7
  61.2 0.0 copy-start.3
  61.2 1.3 convolution_multiply_fusion.1
  62.6 0.0 copy-done.7
  62.6 0.8 copy-done.3
  63.4 1.8 fusion.23
  65.2 0.4 exponential_reduce_fusion
  65.7 7.8 %all-gather.3 = f32[4,1,256]{2,1,0:T(1,128)S(1)} all-gather(f32[1,1,256]{2,1,0:T(1,128)S(1)} %bitcast.43), channel_id=3, replica_groups=mesh['parts'=2,'mp'=4,'dp'=4] {'mp'}, dimensions={0}, use_global_device_ids=true | all-gather | bytes 5120 | tf_op jit(solution)/shard_map/all_gather | solution.py:8
  73.5 5.8 %all-gather.2 = f32[4,1,256]{2,1,0:T(1,128)S(1)} all-gather(f32[1,1,256]{2,1,0:T(1,128)S(1)} %bitcast.42), channel_id=2, replica_groups=mesh['parts'=2,'mp'=4,'dp'=4] {'mp'}, dimensions={0}, use_global_device_ids=true | all-gather | bytes 5120 | tf_op jit(solution)/shard_map/all_gather | solution.py:8
  79.4 0.1 while.17
  79.5 0.0 copy-start.4
  79.5 0.4 fusion.6
  79.9 0.0 copy-start.5
  80.0 0.0 copy-start.2
  80.0 4.0 %convolution_multiply_fusion.2 = f32[256,1024]{1,0:T(8,128)S(1)} fusion(bf16[256,2048]{1,0:T(8,128)(2,1)S(1)} %get-tuple-element.169, bf16[2048,1024]{1,0:T(8,128)(2,1)} %param.12, bf16[256,1024]{1,0:T(8,128)(2,1)S(1)} %all-reduce.7), kind=kOutput, calls=%fused_computation.29 | convolution fusion | flops 1074266112 | bytes 6815744 | tf_op jit(solution)/shard_map/dot_general | solution.py:65
  84.0 0.0 copy-done.5
  84.0 0.0 copy-done.4
  84.0 0.6 copy-done.2
  84.7 2.1 fusion.14
  86.8 0.0 all-reduce.4.cloned.1.call-update
  86.8 0.0 copy-start.6
  86.8 0.2 reduce-scatter.3.cloned.1.call-start
  87.0 4.6 %convolution_convert_fusion.1 = bf16[1024,2048]{1,0:T(8,128)(2,1)} fusion(bf16[256,2048]{1,0:T(8,128)(2,1)} %copy-done.5, bf16[256,1024]{1,0:T(8,128)(2,1)S(1)} %all-reduce.7), kind=kOutput, calls=%fused_computation.14 | convolution fusion | flops 1076625408 | bytes 5767168 | tf_op jit(solution)/shard_map/dot_general | solution.py:56
  91.6 0.0 copy-done.6
  91.6 3.3 %convolution_convert_fusion.2 = bf16[1024,2048]{1,0:T(8,128)(2,1)} fusion(bf16[256,1024]{1,0:T(8,128)(2,1)S(1)} %all-reduce.7, bf16[256,2048]{1,0:T(8,128)(2,1)S(1)} %copy-done.6), kind=kOutput, calls=%fused_computation.15 | convolution fusion | flops 1075838976 | bytes 5767168 | tf_op jit(solution)/shard_map/dot_general | solution.py:55
  94.8 7.8 %pad_maximum_fusion = bf16[1024,4096]{1,0:T(8,128)(2,1)} fusion(bf16[1024,2048]{1,0:T(8,128)(2,1)} %convolution_convert_fusion.1, bf16[1024,2048]{1,0:T(8,128)(2,1)} %convolution_convert_fusion.2), kind=kLoop, calls=%fused_computation.10 | loop fusion | flops 16777216 | bytes 16777216 | tf_op jit(solution)/shard_map/concatenate | solution.py:58
  102.6 0.0 reduce-scatter.3.cloned.1.call-update
  102.7 0.0 reduce-scatter.5.cloned.1.call-start
  102.7 28.5 %all-reduce.4.cloned.1.call-done = bf16[256,1024]{1,0:T(8,128)(2,1)} async-done(((bf16[256,1024]{1,0:T(8,128)(2,1)}), bf16[256,1024]{1,0:T(8,128)(2,1)}) %all-reduce.4.cloned.1.call-update) | async-done | bytes 524304 | tf_op jit(solution)/shard_map/psum | solution.py:68
  131.2 5.3 %fusion.5 = bf16[256,2048]{1,0:T(8,128)(2,1)S(1)} fusion(bf16[256,1024]{1,0:T(8,128)(2,1)} %all-reduce.4.cloned.1.call-done, bf16[2048,1024]{1,0:T(8,128)(2,1)} %param.10, f32[256,2048]{1,0:T(8,128)} %copy-done.10), kind=kOutput, calls=%fused_computation.21 | convolution fusion | flops 1078460416 | bytes 7864320 | tf_op jit(solution)/shard_map/dot_general | solution.py:69
  136.4 0.0 copy-start.9
  136.4 0.0 copy-start.11
  136.5 3.2 %convert_bitcast_fusion = bf16[1024,2048]{0,1:T(8,128)(2,1)} fusion(bf16[256,2048]{1,0:T(8,128)(2,1)S(1)} %fusion.5, bf16[256,1024]{1,0:T(8,128)(2,1)S(1)} %copy-done), kind=kOutput, calls=%fused_computation.12 | convolution fusion | flops 1075838976 | bytes 5767168 | tf_op jit(solution)/shard_map/dot_general | solution.py:75
  139.7 0.0 copy-done.9
  139.7 0.0 copy-done.11
  139.7 3.4 %convolution_convert_fusion = bf16[1024,2048]{0,1:T(8,128)(2,1)} fusion(bf16[256,1024]{1,0:T(8,128)(2,1)S(1)} %copy-done.9, f32[256,2048]{1,0:T(8,128)S(1)} %copy-done.11), kind=kOutput, calls=%fused_computation.13 | convolution fusion | flops 1078460416 | bytes 6815744 | tf_op jit(solution)/shard_map/dot_general | solution.py:78
  143.1 7.7 %pad_maximum_fusion.1 = bf16[1024,4096]{0,1:T(8,128)(2,1)} fusion(bf16[1024,2048]{0,1:T(8,128)(2,1)} %convolution_convert_fusion, bf16[1024,2048]{0,1:T(8,128)(2,1)} %convert_bitcast_fusion), kind=kLoop, calls=%fused_computation.11 | loop fusion | flops 16777216 | bytes 16777216 | tf_op jit(solution)/shard_map/concatenate | solution.py:80
  150.8 0.0 reduce-scatter.5.cloned.1.call-update
  150.8 0.0 all-reduce.6.cloned.1.call-start
  150.9 7.6 %psum.29 = f32[2048]{0:T(1024)} all-reduce(f32[2048]{0:T(1024)S(1)} %get-tuple-element.170), channel_id=1, replica_groups=mesh['parts'=2,'mp'=4,'dp'=4] {'dp'}, use_global_device_ids=true, to_apply=%region_8.9 | all-reduce | flops 2048 | bytes 16384 | tf_op jit(solution)/shard_map/psum | solution.py:53
  158.4 4.3 %convolution_convert_fusion.3 = bf16[256,1024]{1,0:T(8,128)(2,1)} fusion(bf16[256,2048]{1,0:T(8,128)(2,1)S(1)} %fusion.5, bf16[1024,2048]{1,0:T(8,128)(2,1)} %param.9), kind=kOutput, calls=%fused_computation.33 | convolution fusion | flops 1074003968 | bytes 5767168 | tf_op jit(solution)/shard_map/dot_general | solution.py:72
  162.7 0.0 all-reduce.6.cloned.1.call-update
  162.7 18.0 %reduce-scatter.3.cloned.1.call-done = bf16[256,4096]{1,0:T(8,128)(2,1)} async-done(((bf16[1024,4096]{1,0:T(8,128)(2,1)}), bf16[256,4096]{1,0:T(8,128)(2,1)}) %reduce-scatter.3.cloned.1.call-update) | async-done | bytes 2097168 | tf_op jit(solution)/shard_map/reduce_scatter | solution.py:57
  180.7 4.1 %fusion.22 = (f32[256,2048]{1,0:T(8,128)}, f32[256,2048]{1,0:T(8,128)}) fusion(bf16[256,4096]{1,0:T(8,128)(2,1)} %reduce-scatter.3.cloned.1.call-done), kind=kLoop, calls=%fused_computation.41 | loop fusion | bytes 8388608 | tf_op jit(solution)/shard_map/slice | solution.py:64
  184.8 69.5 %reduce-scatter.5.cloned.1.call-done = bf16[256,4096]{0,1:T(8,128)(2,1)} async-done(((bf16[1024,4096]{0,1:T(8,128)(2,1)}), bf16[256,4096]{0,1:T(8,128)(2,1)}) %reduce-scatter.5.cloned.1.call-update) | async-done | bytes 2097168 | tf_op jit(solution)/shard_map/reduce_scatter | solution.py:79
  254.3 1.7 fusion.21
  256.0 1.4 copy.17
  257.4 1.4 copy.16
  258.8 0.0 all-reduce.6.cloned.1.call-done
  258.8 1.9 copy.38
  (12 shorter events, 0.1 us)
Async XLA Ops:
  8.0 1.0 copy-start
  8.0 123.2 %all-reduce.4.cloned.1.call-start = ((), (), s32[]{:S(2)}) async-start(), calls=%async_computation.3 | async-start | bytes 1048576 | tf_op jit(solution)/shard_map/psum | solution.py:68
  9.0 4.9 %copy-start.8 = (bf16[2048,1024]{1,0:T(8,128)(2,1)S(1)}, bf16[2048,1024]{1,0:T(8,128)(2,1)}, u32[]{:S(2)}) copy-start(bf16[2048,1024]{1,0:T(8,128)(2,1)} %param.10) | copy-start | bytes 12582916
  12.6 1.3 copy-start.10
  55.9 5.3 %copy-start.1 = (bf16[2048,1024]{1,0:T(8,128)(2,1)S(1)}, bf16[2048,1024]{1,0:T(8,128)(2,1)}, u32[]{:S(2)}) copy-start(bf16[2048,1024]{1,0:T(8,128)(2,1)} %param.12) | copy-start | bytes 12582916
  61.2 1.4 copy-start.7
  61.2 2.2 copy-start.3
  79.5 4.5 %copy-start.4 = (bf16[2048,1024]{1,0:T(8,128)(2,1)S(1)}, bf16[2048,1024]{1,0:T(8,128)(2,1)}, u32[]{:S(2)}) copy-start(bf16[2048,1024]{1,0:T(8,128)(2,1)} %param.11) | copy-start | bytes 12582916
  79.9 4.1 %copy-start.5 = (bf16[256,2048]{1,0:T(8,128)(2,1)}, bf16[256,2048]{1,0:T(8,128)(2,1)S(1)}, u32[]{:S(2)}) copy-start(bf16[256,2048]{1,0:T(8,128)(2,1)S(1)} %get-tuple-element.169) | copy-start | bytes 3145732
  80.0 4.7 %copy-start.2 = (bf16[2048,1024]{1,0:T(8,128)(2,1)S(1)}, bf16[2048,1024]{1,0:T(8,128)(2,1)}, u32[]{:S(2)}) copy-start(bf16[2048,1024]{1,0:T(8,128)(2,1)} %param.12) | copy-start | bytes 12582916
  86.8 4.8 %copy-start.6 = (bf16[256,2048]{1,0:T(8,128)(2,1)S(1)}, bf16[256,2048]{1,0:T(8,128)(2,1)}, u32[]{:S(2)}) copy-start(bf16[256,2048]{1,0:T(8,128)(2,1)} %copy-done.5) | copy-start | bytes 3145732
  86.8 93.9 %reduce-scatter.3.cloned.1.call-start = ((), (), s32[]{:S(2)}) async-start(), calls=%async_computation.2 | async-start | bytes 10485760 | tf_op jit(solution)/shard_map/reduce_scatter | solution.py:57
  102.7 151.6 %reduce-scatter.5.cloned.1.call-start = ((), (), s32[]{:S(2)}) async-start(), calls=%async_computation.4 | async-start | bytes 10485760 | tf_op jit(solution)/shard_map/reduce_scatter | solution.py:79
  136.4 3.2 %copy-start.9 = (bf16[256,1024]{1,0:T(8,128)(2,1)S(1)}, bf16[256,1024]{1,0:T(8,128)(2,1)}, u32[]{:S(2)}) copy-start(bf16[256,1024]{1,0:T(8,128)(2,1)} %all-reduce.4.cloned.1.call-done) | copy-start | bytes 1572868
  136.4 3.2 %copy-start.11 = (f32[256,2048]{1,0:T(8,128)S(1)}, f32[256,2048]{1,0:T(8,128)}, u32[]{:S(2)}) copy-start(f32[256,2048]{1,0:T(8,128)} %copy-done.10) | copy-start | bytes 6291460
  150.8 108.0 %all-reduce.6.cloned.1.call-start = ((), (), s32[]{:S(2)}) async-start(), calls=%async_computation.5 | async-start | bytes 1048576 | tf_op jit(solution)/shard_map/psum | solution.py:73
Sparse Core Ops, SparseCore 0:
  86.9 44.2 all-reduce.3
  162.9 38.2 all-reduce.5
Sparse Core Ops, SparseCore 1:
  102.7 77.9 reduce-scatter.2
  183.2 71.0 reduce-scatter.4
where the time goes:
time: 269 us; the launch traced here: 268 us
  waiting for transfers between devices  116 us (43%)
  blocking collectives  61.9 us (23%)
  matrix products  38.2 us (14%)
  other arithmetic  21.6 us (8%)
  between operations  15.7 us (6%)
  local copies, waits for them, and re-layouts  14.3 us (5%)
    reduce_scatter x1, waiting for transfers between devices, body(): lax.psum_scatter(jnp.concatenate([term_in, term_out], axis=1).astype(jnp....  69.5 us
    psum x1, blocking collectives, body(): head = lax.psum(partial_value, 'mp').astype(jnp.bfloat16)  40.6 us
    psum x1, waiting for transfers between devices, body(): grad_head = lax.psum(grad_term.astype(jnp.bfloat16), 'mp')  28.5 us
    reduce_scatter x1, waiting for transfers between devices, body(): lax.psum_scatter(jnp.concatenate([first, second], axis=1).astype(jnp.bflo...  18 us
    all_gather x2, blocking collectives, combined_all(): gathered = jax.tree.map(lambda a: lax.all_gather(a, axis), part)  13.7 us
    unnamed x29, local copies, waits for them, and re-layouts  8.52 us
    concatenate x1, other arithmetic, body(): jnp.concatenate([first, second], axis=1).astype(jnp.bfloat16)  7.8 us
    concatenate x1, other arithmetic, body(): jnp.concatenate([term_in, term_out], axis=1).astype(jnp.bfloat16)  7.65 us
  transfers between devices with their start and end apart: 4, of which 3 were waited for; matrix products, arithmetic and copies ran while one was open for 18% of the time, Pallas kernels for 0%

commit v1 on v0

v1 whole, which is shorter than its diff:
```python
import jax
import jax.numpy as jnp
from jax import lax
from jax.sharding import PartitionSpec as P


def my_columns(rows, axis):
    gathered = lax.all_gather(rows, axis, axis=0, tiled=True)
    width = rows.shape[1] // lax.axis_size(axis)
    return lax.dynamic_slice_in_dim(gathered, lax.axis_index(axis) * width, width, 1)


def body(embeddings, w_in, w_out, means, precisions, log_weight):
    contract_rows = (((0,), (0,)), ((), ()))
    contract_cols = (((1,), (1,)), ((), ()))
    pre = jnp.dot(embeddings, w_in, preferred_element_type=jnp.float32)
    hidden = jax.nn.silu(pre).astype(jnp.bfloat16)
    hidden_all = lax.all_gather(hidden, "dp", axis=0, tiled=True)
    emb_cols = my_columns(embeddings, "dp")
    partial_value = jnp.dot(hidden, w_out, preferred_element_type=jnp.float32)
    head = lax.psum(partial_value, "mp").astype(jnp.bfloat16)
    head_f = head.astype(jnp.float32)
    squares = (head_f * head_f).astype(jnp.bfloat16)
    means_f = means.astype(jnp.float32)
    prec_f = precisions.astype(jnp.float32)
    weighted = (means_f * prec_f).astype(jnp.bfloat16)
    offset = (
        log_weight
        + 0.5 * jnp.sum(jnp.log(prec_f), axis=1)
        - 0.5 * jnp.sum(means_f * means_f * prec_f, axis=1)
    )
    scores = offset[None, :] + lax.dot_general(
        head, weighted, contract_cols, preferred_element_type=jnp.float32
    )
    scores = scores - 0.5 * lax.dot_general(
        squares, precisions, contract_cols, preferred_element_type=jnp.float32
    )
    local_top = jnp.max(scores, axis=1)
    local_total = jnp.sum(jnp.exp(scores - local_top[:, None]), axis=1)
    stats = lax.all_gather(jnp.stack([local_top, local_total]), "mp")
    top = jnp.max(stats[:, 0], axis=0)
    total = jnp.sum(stats[:, 1] * jnp.exp(stats[:, 0] - top), axis=0)
    lse = top + jnp.log(total)
    resp = jnp.exp(scores - lse[:, None])
    resp_b = resp.astype(jnp.bfloat16)
    counts = lax.psum(jnp.sum(resp, axis=0), "dp")
    resp_all = lax.all_gather(resp_b, "dp", axis=0, tiled=True)
    head_cols = my_columns(head, "dp")
    head_cols_f = head_cols.astype(jnp.float32)
    squares_cols = (head_cols_f * head_cols_f).astype(jnp.bfloat16)
    first_moment = lax.dot_general(
        head_cols, resp_all, contract_rows, preferred_element_type=jnp.float32
    )
    second_moment = lax.dot_general(
        squares_cols, resp_all, contract_rows, preferred_element_type=jnp.float32
    )
    along = jnp.dot(resp_b, precisions, preferred_element_type=jnp.float32)
    shifted = jnp.dot(resp_b, weighted, preferred_element_type=jnp.float32)
    grad_term = head_f * along - shifted
    grad_head = lax.psum(grad_term.astype(jnp.bfloat16), "mp")
    back = lax.dot_general(grad_head, w_out, contract_cols, preferred_element_type=jnp.float32)
    sigma = jax.nn.sigmoid(pre)
    grad_pre = (back * sigma * (1.0 + pre * (1.0 - sigma))).astype(jnp.bfloat16)
    embed_term = lax.dot_general(grad_pre, w_in, contract_cols, preferred_element_type=jnp.float32)
    grad_embed = lax.psum(embed_term.astype(jnp.bfloat16), "mp")
    pre_all = lax.all_gather(grad_pre, "dp", axis=0, tiled=True)
    grad_cols = my_columns(grad_head, "dp")
    grad_w_in = lax.dot_general(
        emb_cols, pre_all, contract_rows, preferred_element_type=jnp.float32
    ).astype(jnp.bfloat16)
    grad_w_out_t = lax.dot_general(
        grad_cols, hidden_all, contract_rows, preferred_element_type=jnp.float32
    ).astype(jnp.bfloat16)
    return (counts, first_moment, second_moment, grad_w_in, grad_w_out_t, grad_embed)


def solution(mesh):
    return jax.shard_map(
        body,
        mesh=mesh,
        in_specs=(
            P(("parts", "dp"), None),
            P(None, "mp"),
            P("mp", None),
            P("mp", None),
            P("mp", None),
            P("mp"),
        ),
        out_specs=(
            P(("parts", "mp")),
            P(("parts", "dp"), "mp"),
            P(("parts", "dp"), "mp"),
            P(("parts", "dp"), "mp"),
            P(("parts", "dp"), "mp"),
            P(("parts", "dp"), None),
        ),
        check_vma=False,
    )
```

time: 269 us -> 289 us (1.074)
  waiting for transfers between devices: 116 us -> 156 us
  other arithmetic: 21.6 us -> 5.57 us
  local copies, waits for them, and re-layouts: 14.3 us -> 1.92 us
  matrix products: 38.2 us -> 50.5 us
  blocking collectives: 61.9 us -> 57.7 us
    all_gather x0 -> x6, waiting for transfers between devices: none -> 112 us  [the longest x1 36.5 us: body(): pre_all = lax.all_gather(grad_pre, 'dp', axis=0, tiled=True)]
    reduce_scatter x2 -> x0, waiting for transfers between devices: 87.5 us -> none  [the longest x1 69.5 us: body(): lax.psum_scatter(jnp.concatenate([term_in, term_out], axis=1).astype(jnp....]
    concatenate x2 -> x0, other arithmetic: 15.5 us -> none  [the longest x1 7.8 us: body(): jnp.concatenate([first, second], axis=1).astype(jnp.bfloat16)]
    psum x1, waiting for transfers between devices: 28.5 us -> 41.8 us  [body(): grad_head = lax.psum(grad_term.astype(jnp.bfloat16), 'mp')]
    unnamed x29 -> x19, local copies, waits for them, and re-layouts: 8.52 us -> 1.92 us
    slice x2 -> x0, local copies, waits for them, and re-layouts: 5.77 us -> none  [the longest x1 4.09 us: body(): second_moment = moments[:, local_comp:]]
    all_gather x2 -> x1, blocking collectives: 13.7 us -> 9.34 us  [body(): stats = lax.all_gather(jnp.stack([local_top, local_total]), 'mp')]
    dot_general x4, matrix products: 14.5 us -> 18 us  [the longest x1 5.2 us: body(): lax.dot_general(squares_cols, resp_all, contract_rows, preferred_element_...]
  transfers between devices with their start and end apart: 4 -> 8, of which waited for: 3 -> 6; matrix products, arithmetic and copies ran while one was open for 18% -> 10% of each run, Pallas kernels for 0% -> 0%
where the time goes in v1:
time: 289 us; the launch traced here: 288 us
  waiting for transfers between devices  156 us (54%)
  blocking collectives  57.7 us (20%)
  matrix products  50.5 us (17%)
  between operations  15.8 us (5%)
  other arithmetic  5.57 us (2%)
    psum x1, waiting for transfers between devices, body(): grad_head = lax.psum(grad_term.astype(jnp.bfloat16), 'mp')  41.8 us
    psum x1, blocking collectives, body(): head = lax.psum(partial_value, 'mp').astype(jnp.bfloat16)  40.6 us
    all_gather x1, waiting for transfers between devices, body(): pre_all = lax.all_gather(grad_pre, 'dp', axis=0, tiled=True)  36.5 us
    all_gather x1, waiting for transfers between devices, body(): hidden_all = lax.all_gather(hidden, 'dp', axis=0, tiled=True)  35.9 us
    all_gather x3, waiting for transfers between devices, my_columns(): gathered = lax.all_gather(rows, axis, axis=0, tiled=True)  34.5 us
    all_gather x1, blocking collectives, body(): stats = lax.all_gather(jnp.stack([local_top, local_total]), 'mp')  9.34 us
    psum x1, blocking collectives, body(): counts = lax.psum(jnp.sum(resp, axis=0), 'dp')  7.82 us
  transfers between devices with their start and end apart: 8, of which 6 were waited for; matrix products, arithmetic and copies ran while one was open for 10% of the time, Pallas kernels for 0%

profile of v1, /device:TPU:1, one launch (start us, length us, event | category | flops | bytes accessed | tf_op | source)
XLA Modules:
  0.0 288.2 jit_solution(5527400726379757286)
XLA Ops:
  8.0 0.0 all-reduce.4.cloned.1.call-start
  8.0 5.0 %multiply_convert_fusion = (bf16[256,2048]{1,0:T(8,128)(2,1)S(1)}, f32[256,2048]{1,0:T(8,128)}) fusion(bf16[256,1024]{1,0:T(8,128)(2,1)} %param.6, bf16[1024,2048]{1,0:T(8,128)(2,1)} %param.7), kind=kOutput, calls=%fused_computation.17 | convolution fusion | flops 1076363264 | bytes 7864320 | tf_op jit(solution)/shard_map/dot_general | solution.py:16
  13.0 0.0 copy-start.5
  13.0 3.8 %fusion.34 = f32[256,1024]{1,0:T(8,128)S(1)} fusion(bf16[256,2048]{1,0:T(8,128)(2,1)S(1)} %get-tuple-element.13, bf16[2048,1024]{1,0:T(8,128)(2,1)} %param.8), kind=kOutput, calls=%fused_computation.50 | convolution fusion | flops 1073741824 | bytes 6291456 | tf_op jit(solution)/shard_map/dot_general | solution.py:20
  16.9 40.6 %all-reduce.7 = bf16[256,1024]{1,0:T(8,128)(2,1)S(1)} all-reduce(f32[256,1024]{1,0:T(8,128)S(1)} %fusion.34), channel_id=1, replica_groups=mesh['parts'=2,'mp'=4,'dp'=4] {'mp'}, use_global_device_ids=true, to_apply=%region_2.3 | all-reduce | flops 262144 | bytes 1572864 | tf_op jit(solution)/shard_map/psum | solution.py:21
  57.5 0.0 copy-done.5
  57.5 0.0 copy-start.4
  57.5 0.0 copy-start
  57.5 3.7 %convolution_multiply_fusion.1 = f32[256,2048]{1,0:T(8,128)S(1)} fusion(bf16[2048,1024]{1,0:T(8,128)(2,1)} %param.10, bf16[256,1024]{1,0:T(8,128)(2,1)S(1)} %all-reduce.7), kind=kOutput, calls=%fused_computation.8 | convolution fusion | flops 1075052544 | bytes 6815744 | tf_op jit(solution)/shard_map/dot_general | solution.py:35
  61.2 0.0 copy-done
  61.2 0.0 copy-start.6
  61.2 0.0 copy-start.2
  61.2 4.7 %fusion = (f32[2048]{0:T(1024)S(1)}, f32[2048]{0:T(1024)S(1)}) fusion(bf16[2048,1024]{1,0:T(8,128)(2,1)S(1)} %copy-done, bf16[2048,1024]{1,0:T(8,128)(2,1)} %param.9), kind=kLoop, calls=%fused_computation.4 | loop fusion | flops 12578816 | bytes 8404992 | tf_op jit(solution)/shard_map/reduce_sum | solution.py:29
  65.9 0.0 copy-done.6
  65.9 0.0 copy-done.2
  65.9 1.9 fusion.33
  67.8 0.4 exponential_reduce_fusion
  68.2 9.3 %all-gather.1 = f32[4,2,256]{2,1,0:T(2,128)S(1)} all-gather(f32[1,2,256]{2,1,0:T(2,128)S(1)} %maximum_bitcast_fusion), channel_id=2, replica_groups=mesh['parts'=2,'mp'=4,'dp'=4] {'mp'}, dimensions={0}, use_global_device_ids=true | all-gather | bytes 10240 | tf_op jit(solution)/shard_map/all_gather | solution.py:40
  77.7 0.4 fusion.6
  78.1 0.0 copy-start.3
  78.1 0.0 copy-done.4
  78.1 0.0 copy-start.1
  78.1 3.9 %convolution_multiply_fusion.2 = f32[256,1024]{1,0:T(8,128)S(1)} fusion(bf16[256,2048]{1,0:T(8,128)(2,1)S(1)} %get-tuple-element.8, bf16[2048,1024]{1,0:T(8,128)(2,1)} %param.10, bf16[256,1024]{1,0:T(8,128)(2,1)S(1)} %all-reduce.7), kind=kOutput, calls=%fused_computation.22 | convolution fusion | flops 1074266112 | bytes 6815744 | tf_op jit(solution)/shard_map/dot_general | solution.py:57
  82.0 0.0 copy-done.1
  82.0 4.6 %fusion.14 = bf16[256,1024]{1,0:T(8,128)(2,1)} fusion(f32[256,1024]{1,0:T(8,128)S(1)} %convolution_multiply_fusion.2, bf16[256,2048]{1,0:T(8,128)(2,1)S(1)} %get-tuple-element.8, bf16[2048,1024]{1,0:T(8,128)(2,1)S(1)} %copy-done.1, bf16[2048,1024]{1,0:T(8,128)(2,1)} %param.9), kind=kOutput, calls=%fused_computation.25 | convolution fusion | flops 1082654720 | bytes 11010048 | tf_op jit(solution)/shard_map/dot_general | solution.py:58
  86.6 0.0 copy-done.3
  86.6 0.0 copy-start.8
  86.6 0.0 all-reduce.4.cloned.1.call-update
  86.6 0.0 all-gather.9.cloned.1.call-start
  86.7 0.5 all-gather.9.cloned.1.call-update
  87.2 0.0 all-gather.11.cloned.1.call-start
  87.3 0.5 all-gather.11.cloned.1.call-update
  87.8 0.0 all-gather.17.cloned.1.call-start
  87.9 41.8 %all-reduce.4.cloned.1.call-done = bf16[256,1024]{1,0:T(8,128)(2,1)} async-done(((bf16[256,1024]{1,0:T(8,128)(2,1)}), bf16[256,1024]{1,0:T(8,128)(2,1)}) %all-reduce.4.cloned.1.call-update) | async-done | bytes 524304 | tf_op jit(solution)/shard_map/psum | solution.py:60
  129.6 0.0 all-gather.17.cloned.1.call-update
  129.6 0.0 all-gather.19.cloned.1.call-start
  129.7 0.7 all-gather.19.cloned.1.call-update
  130.4 0.0 all-gather.13.cloned.1.call-start
  130.4 0.7 all-gather.13.cloned.1.call-update
  131.1 0.0 all-gather.15.cloned.1.call-start
  131.2 0.0 copy-done.8
  131.2 5.0 %fusion.5 = bf16[256,2048]{1,0:T(8,128)(2,1)} fusion(bf16[256,1024]{1,0:T(8,128)(2,1)} %all-reduce.4.cloned.1.call-done, bf16[2048,1024]{1,0:T(8,128)(2,1)} %param.8, f32[256,2048]{1,0:T(8,128)S(1)} %copy-done.8), kind=kOutput, calls=%fused_computation.12 | convolution fusion | flops 1078460416 | bytes 7864320 | tf_op jit(solution)/shard_map/dot_general | solution.py:61
  136.2 0.0 all-gather.15.cloned.1.call-update
  136.2 0.0 all-reduce.6.cloned.1.call-start
  136.3 7.8 %psum.29 = f32[2048]{0:T(1024)} all-reduce(f32[2048]{0:T(1024)S(1)} %get-tuple-element.9), channel_id=1, replica_groups=mesh['parts'=2,'mp'=4,'dp'=4] {'dp'}, use_global_device_ids=true, to_apply=%region_8.9 | all-reduce | flops 2048 | bytes 16384 | tf_op jit(solution)/shard_map/psum | solution.py:46
  144.1 4.6 %convolution_convert_fusion.2 = bf16[256,1024]{1,0:T(8,128)(2,1)} fusion(bf16[256,2048]{1,0:T(8,128)(2,1)} %fusion.5, bf16[1024,2048]{1,0:T(8,128)(2,1)} %param.7), kind=kOutput, calls=%fused_computation.26 | convolution fusion | flops 1074003968 | bytes 5767168 | tf_op jit(solution)/shard_map/dot_general | solution.py:64
  148.7 0.0 all-reduce.6.cloned.1.call-update
  148.7 0.0 all-gather.9.cloned.1.call-done
  148.7 5.2 %all-gather.11.cloned.1.call-done = bf16[1024,2048]{1,0:T(8,128)(2,1)} async-done(((bf16[256,2048]{1,0:T(8,128)(2,1)}), bf16[1024,2048]{1,0:T(8,128)(2,1)}) %all-gather.11.cloned.1.call-update) | async-done | bytes 4194320 | tf_op jit(solution)/shard_map/all_gather | solution.py:47
  153.9 0.0 copy-start.7
  153.9 5.2 %fusion.18 = f32[256,2048]{1,0:T(8,128)} fusion(bf16[1024,2048]{1,0:T(8,128)(2,1)} %all-gather.11.cloned.1.call-done, bf16[1024,1024]{1,0:T(8,128)(2,1)} %all-gather.9.cloned.1.call-done, s32[]{:T(128)S(6)} %select_n.2), kind=kOutput, calls=%fused_computation.29 | convolution fusion | flops 1074528256 | bytes 6815748 | tf_op jit(solution)/shard_map/dot_general | solution.py:54
  159.1 0.0 copy-done.7
  159.1 3.6 %fusion.23 = f32[256,2048]{1,0:T(8,128)} fusion(bf16[1024,2048]{1,0:T(8,128)(2,1)S(1)} %copy-done.7, bf16[1024,1024]{1,0:T(8,128)(2,1)} %all-gather.9.cloned.1.call-done, s32[]{:T(128)S(6)} %select_n.2), kind=kOutput, calls=%fused_computation.33 | convolution fusion | flops 1073741824 | bytes 6815748 | tf_op jit(solution)/shard_map/dot_general | solution.py:51
  162.7 15.0 %all-gather.17.cloned.1.call-done = bf16[1024,1024]{1,0:T(8,128)(2,1)} async-done(((bf16[256,1024]{1,0:T(8,128)(2,1)}), bf16[1024,1024]{1,0:T(8,128)(2,1)}) %all-gather.17.cloned.1.call-update) | async-done | bytes 2097168 | tf_op jit(solution)/shard_map/all_gather | solution.py:8
  177.8 35.9 %all-gather.19.cloned.1.call-done = bf16[1024,2048]{1,0:T(8,128)(2,1)} async-done(((bf16[256,2048]{1,0:T(8,128)(2,1)}), bf16[1024,2048]{1,0:T(8,128)(2,1)}) %all-gather.19.cloned.1.call-update) | async-done | bytes 4194320 | tf_op jit(solution)/shard_map/all_gather | solution.py:18
  213.7 4.6 %convolution_convert_fusion = bf16[256,2048]{1,0:T(8,128)(2,1)} fusion(bf16[1024,2048]{1,0:T(8,128)(2,1)} %all-gather.19.cloned.1.call-done, bf16[1024,1024]{1,0:T(8,128)(2,1)} %all-gather.17.cloned.1.call-done, s32[]{:T(128)S(6)} %select_n.2), kind=kOutput, calls=%fused_computation.13 | convolution fusion | flops 1074266112 | bytes 5767172 | tf_op jit(solution)/shard_map/dot_general | solution.py:71
  218.3 19.4 %all-gather.13.cloned.1.call-done = bf16[1024,1024]{1,0:T(8,128)(2,1)} async-done(((bf16[256,1024]{1,0:T(8,128)(2,1)}), bf16[1024,1024]{1,0:T(8,128)(2,1)}) %all-gather.13.cloned.1.call-update) | async-done | bytes 2097168 | tf_op jit(solution)/shard_map/all_gather | solution.py:8
  237.8 36.5 %all-gather.15.cloned.1.call-done = bf16[1024,2048]{1,0:T(8,128)(2,1)} async-done(((bf16[256,2048]{1,0:T(8,128)(2,1)}), bf16[1024,2048]{1,0:T(8,128)(2,1)}) %all-gather.15.cloned.1.call-update) | async-done | bytes 4194320 | tf_op jit(solution)/shard_map/all_gather | solution.py:66
  274.3 4.6 %convolution_convert_fusion.1 = bf16[256,2048]{1,0:T(8,128)(2,1)} fusion(bf16[1024,2048]{1,0:T(8,128)(2,1)} %all-gather.15.cloned.1.call-done, bf16[1024,1024]{1,0:T(8,128)(2,1)} %all-gather.13.cloned.1.call-done, s32[]{:T(128)S(6)} %select_n.2), kind=kOutput, calls=%fused_computation.14 | convolution fusion | flops 1074266112 | bytes 5767172 | tf_op jit(solution)/shard_map/dot_general | solution.py:68
  278.9 0.0 all-reduce.6.cloned.1.call-done
  278.9 1.9 copy.26
  (5 shorter events, 0.1 us)
Async XLA Ops:
  8.0 121.6 %all-reduce.4.cloned.1.call-start = ((), (), s32[]{:S(2)}) async-start(), calls=%async_computation.3 | async-start | bytes 1048576 | tf_op jit(solution)/shard_map/psum | solution.py:60
  13.0 44.4 %copy-start.5 = (bf16[256,2048]{1,0:T(8,128)(2,1)}, bf16[256,2048]{1,0:T(8,128)(2,1)S(1)}, u32[]{:S(2)}) copy-start(bf16[256,2048]{1,0:T(8,128)(2,1)S(1)} %get-tuple-element.13) | copy-start | bytes 3145732
  57.5 20.6 %copy-start.4 = (bf16[256,1024]{1,0:T(8,128)(2,1)}, bf16[256,1024]{1,0:T(8,128)(2,1)S(1)}, u32[]{:S(2)}) copy-start(bf16[256,1024]{1,0:T(8,128)(2,1)S(1)} %all-reduce.7) | copy-start | bytes 1572868
  57.5 3.7 %copy-start = (bf16[2048,1024]{1,0:T(8,128)(2,1)S(1)}, bf16[2048,1024]{1,0:T(8,128)(2,1)}, u32[]{:S(2)}) copy-start(bf16[2048,1024]{1,0:T(8,128)(2,1)} %param.10) | copy-start | bytes 12582916
  61.2 4.7 %copy-start.6 = (f32[2048]{0:T(1024)S(1)}, f32[2048]{0:T(1024)}, u32[]{:S(2)}) copy-start(f32[2048]{0:T(1024)} %param.11) | copy-start | bytes 24580
  61.2 4.7 %copy-start.2 = (bf16[2048,1024]{1,0:T(8,128)(2,1)S(1)}, bf16[2048,1024]{1,0:T(8,128)(2,1)}, u32[]{:S(2)}) copy-start(bf16[2048,1024]{1,0:T(8,128)(2,1)} %param.9) | copy-start | bytes 12582916
  78.1 8.6 %copy-start.3 = (bf16[256,2048]{1,0:T(8,128)(2,1)}, bf16[256,2048]{1,0:T(8,128)(2,1)S(1)}, u32[]{:S(2)}) copy-start(bf16[256,2048]{1,0:T(8,128)(2,1)S(1)} %get-tuple-element.8) | copy-start | bytes 3145732
  78.1 3.9 %copy-start.1 = (bf16[2048,1024]{1,0:T(8,128)(2,1)S(1)}, bf16[2048,1024]{1,0:T(8,128)(2,1)}, u32[]{:S(2)}) copy-start(bf16[2048,1024]{1,0:T(8,128)(2,1)} %param.10) | copy-start | bytes 12582916
  86.6 44.6 %copy-start.8 = (f32[256,2048]{1,0:T(8,128)S(1)}, f32[256,2048]{1,0:T(8,128)}, u32[]{:S(2)}) copy-start(f32[256,2048]{1,0:T(8,128)} %get-tuple-element.14) | copy-start | bytes 6291460
  86.6 62.1 %all-gather.9.cloned.1.call-start = ((), (), s32[]{:S(2)}) async-start(), calls=%async_computation | async-start | bytes 2621440 | tf_op jit(solution)/shard_map/all_gather | solution.py:8
  87.2 66.7 %all-gather.11.cloned.1.call-start = ((), (), s32[]{:S(2)}) async-start(), calls=%async_computation.1 | async-start | bytes 5242880 | tf_op jit(solution)/shard_map/all_gather | solution.py:47
  87.8 90.0 %all-gather.17.cloned.1.call-start = ((), (), s32[]{:S(2)}) async-start(), calls=%async_computation.5 | async-start | bytes 2621440 | tf_op jit(solution)/shard_map/all_gather | solution.py:8
  129.6 84.1 %all-gather.19.cloned.1.call-start = ((), (), s32[]{:S(2)}) async-start(), calls=%async_computation.6 | async-start | bytes 5242880 | tf_op jit(solution)/shard_map/all_gather | solution.py:18
  130.4 107.4 %all-gather.13.cloned.1.call-start = ((), (), s32[]{:S(2)}) async-start(), calls=%async_computation.2 | async-start | bytes 2621440 | tf_op jit(solution)/shard_map/all_gather | solution.py:8
  131.1 143.1 %all-gather.15.cloned.1.call-start = ((), (), s32[]{:S(2)}) async-start(), calls=%async_computation.4 | async-start | bytes 5242880 | tf_op jit(solution)/shard_map/all_gather | solution.py:66
  136.2 142.7 %all-reduce.6.cloned.1.call-start = ((), (), s32[]{:S(2)}) async-start(), calls=%async_computation.7 | async-start | bytes 1048576 | tf_op jit(solution)/shard_map/psum | solution.py:65
  153.9 5.2 %copy-start.7 = (bf16[1024,2048]{1,0:T(8,128)(2,1)S(1)}, bf16[1024,2048]{1,0:T(8,128)(2,1)}, u32[]{:S(2)}) copy-start(bf16[1024,2048]{1,0:T(8,128)(2,1)} %all-gather.11.cloned.1.call-done) | copy-start | bytes 12582916
Sparse Core Ops, SparseCore 0:
  86.8 42.8 all-reduce.3
  148.8 38.0 all-reduce.5
Sparse Core Ops, SparseCore 1:
  89.3 28.0 all-gather.8
  119.3 34.6 all-gather.10
  155.3 22.4 all-gather.16
  179.4 34.3 all-gather.18
  215.3 22.4 all-gather.12
  239.9 34.3 all-gather.14

commit v2 on v1

v2 whole, which is shorter than its diff:
```python
import functools

import jax
import jax.numpy as jnp
from jax import lax
from jax.experimental import pallas as pl
from jax.experimental.pallas import tpu as pltpu
from jax.sharding import PartitionSpec as P


def send(src, dst, send_sem, recv_sem, axis, peer):
    return pltpu.make_async_remote_copy(
        src_ref=src,
        dst_ref=dst,
        send_sem=send_sem,
        recv_sem=recv_sem,
        device_id={axis: peer},
        device_id_type=pl.DeviceIdType.MESH,
    )


def greet(groups):
    barrier = pltpu.get_barrier_semaphore()
    count = 0
    for axis, size in groups:
        me = lax.axis_index(axis)
        for step in range(1, size):
            pl.semaphore_signal(
                barrier,
                inc=1,
                device_id={axis: lax.rem(me + step, size)},
                device_id_type=pl.DeviceIdType.MESH,
            )
            count += 1
    pl.semaphore_wait(barrier, count)


def stats_kernel(n, in_ref, out_ref, send_sem, recv_sem):
    greet((("mp", n),))
    me = lax.axis_index("mp")
    copies = []
    for step in range(1, n):
        peer = lax.rem(me + step, n)
        copies.append(
            send(in_ref, out_ref.at[me], send_sem.at[step], recv_sem.at[step], "mp", peer)
        )
        copies[-1].start()
    out_ref[me] = in_ref[...]
    for step in range(1, n):
        copies[step - 1].wait_send()
        source = lax.rem(me + n - step, n)
        send(
            in_ref, out_ref.at[source], send_sem.at[step], recv_sem.at[step], "mp", source
        ).wait_recv()


def gather_stats(stats, n, collective_id):
    return pl.pallas_call(
        functools.partial(stats_kernel, n),
        out_shape=jax.ShapeDtypeStruct((n,) + stats.shape, stats.dtype),
        in_specs=[pl.BlockSpec(memory_space=pltpu.VMEM)],
        out_specs=pl.BlockSpec(memory_space=pltpu.VMEM),
        scratch_shapes=[pltpu.SemaphoreType.DMA((n,)), pltpu.SemaphoreType.DMA((n,))],
        compiler_params=pltpu.CompilerParams(
            collective_id=collective_id, has_side_effects=True, vmem_limit_bytes=4 << 20
        ),
    )(stats)


def exchange_kernel(n_mp, n_dp, pieces, term, block, wide, vec, *refs):
    (total, gathered, columns, vecs, landed) = refs[:5]
    (sum_s, sum_r, out_s, out_r, col_s, col_r, vec_s, vec_r) = refs[5:13]
    (pair_s, pair_r, far_s, far_r, fwd_s, fwd_r, own_sem) = refs[13:]
    greet((("mp", n_mp), ("dp", n_dp)))
    me, dp = lax.axis_index("mp"), lax.axis_index("dp")
    n_x = n_dp // 2
    core, x = lax.rem(dp, 2), lax.div(dp, 2)
    partner = 2 * x + 1 - core
    rows = block.shape[0]
    piece = rows // pieces
    width = wide.shape[1] // n_dp
    sent = []

    def go(*args):
        copy = send(*args)
        copy.start()
        sent.append(copy)

    def arrived(dst, send_sem, recv_sem, axis, peer):
        send(dst, dst, send_sem, recv_sem, axis, peer).wait_recv()

    for step in range(1, n_mp):
        peer = lax.rem(me + step, n_mp)
        go(term.at[peer], landed.at[step], sum_s.at[step], sum_r.at[step], "mp", peer)
    for far in range(1, n_x):
        peer = 2 * lax.rem(x + far, n_x) + core
        for g in range(pieces):
            part = pl.ds(g * piece, piece)
            go(
                block.at[part],
                gathered.at[dp, part],
                far_s.at[far, g],
                far_r.at[far, g],
                "dp",
                peer,
            )
    go(block, gathered.at[dp], pair_s, pair_r, "dp", partner)
    for step in range(1, n_dp):
        peer = lax.rem(dp + step, n_dp)
        cols = pl.ds(pl.multiple_of(peer * width, width), width)
        go(wide.at[:, cols], columns.at[dp], col_s.at[step], col_r.at[step], "dp", peer)
        go(vec, vecs.at[dp], vec_s.at[step], vec_r.at[step], "dp", peer)
    cols = pl.ds(pl.multiple_of(dp * width, width), width)
    own = [
        pltpu.make_async_copy(block, gathered.at[dp], own_sem.at[0]),
        pltpu.make_async_copy(wide.at[:, cols], columns.at[dp], own_sem.at[1]),
        pltpu.make_async_copy(vec, vecs.at[dp], own_sem.at[2]),
    ]
    for copy in own:
        copy.start()

    acc = term[me].astype(jnp.float32)
    for step in range(1, n_mp):
        peer = lax.rem(me + step, n_mp)
        arrived(landed.at[step], sum_s.at[step], sum_r.at[step], "mp", peer)
        acc = acc + landed[step].astype(jnp.float32)
    total[me] = acc.astype(total.dtype)
    for step in range(1, n_mp):
        peer = lax.rem(me + step, n_mp)
        go(total.at[me], total.at[me], out_s.at[step], out_r.at[step], "mp", peer)

    for g in range(pieces):
        part = pl.ds(g * piece, piece)
        for far in range(1, n_x):
            source = 2 * lax.rem(x + n_x - far, n_x) + core
            spot = gathered.at[source, part]
            arrived(spot, far_s.at[far, g], far_r.at[far, g], "dp", source)
            go(spot, spot, fwd_s.at[far, g], fwd_r.at[far, g], "dp", partner)
    arrived(gathered.at[partner], pair_s, pair_r, "dp", partner)
    for step in range(1, n_dp):
        source = lax.rem(dp + n_dp - step, n_dp)
        arrived(columns.at[source], col_s.at[step], col_r.at[step], "dp", source)
        arrived(vecs.at[source], vec_s.at[step], vec_r.at[step], "dp", source)
    for g in range(pieces):
        part = pl.ds(g * piece, piece)
        for far in range(1, n_x):
            source = 2 * lax.rem(x + n_x - far, n_x) + 1 - core
            arrived(
                gathered.at[source, part], fwd_s.at[far, g], fwd_r.at[far, g], "dp", partner
            )
    for step in range(1, n_mp):
        source = lax.rem(me + n_mp - step, n_mp)
        arrived(total.at[source], out_s.at[step], out_r.at[step], "mp", source)
    for copy in own:
        copy.wait()
    for copy in sent:
        copy.wait_send()


def exchange(term, block, wide, vec, n_mp, n_dp, collective_id):
    pieces = 4 if block.shape[0] % 64 == 0 else 1
    rows, width = wide.shape[0], wide.shape[1] // n_dp
    dma = pltpu.SemaphoreType.DMA
    chunk = (n_mp, term.shape[0] // n_mp, term.shape[1])
    vmem = pl.BlockSpec(memory_space=pltpu.VMEM)
    total, gathered, columns, vecs = pl.pallas_call(
        functools.partial(exchange_kernel, n_mp, n_dp, pieces),
        out_shape=(
            jax.ShapeDtypeStruct(chunk, term.dtype),
            jax.ShapeDtypeStruct((n_dp,) + block.shape, block.dtype),
            jax.ShapeDtypeStruct((n_dp, rows, width), wide.dtype),
            jax.ShapeDtypeStruct((n_dp,) + vec.shape, vec.dtype),
        ),
        in_specs=[vmem] * 4,
        out_specs=(vmem,) * 4,
        scratch_shapes=[
            pltpu.VMEM(chunk, term.dtype),
            dma((n_mp,)),
            dma((n_mp,)),
            dma((n_mp,)),
            dma((n_mp,)),
            dma((n_dp,)),
            dma((n_dp,)),
            dma((n_dp,)),
            dma((n_dp,)),
            dma,
            dma,
            dma((n_dp // 2, pieces)),
            dma((n_dp // 2, pieces)),
            dma((n_dp // 2, pieces)),
            dma((n_dp // 2, pieces)),
            dma((3,)),
        ],
        compiler_params=pltpu.CompilerParams(
            collective_id=collective_id, has_side_effects=True, vmem_limit_bytes=20 << 20
        ),
    )(term.reshape(chunk), block, wide, vec)
    return (
        total.reshape(term.shape),
        gathered.reshape(n_dp * block.shape[0], block.shape[1]),
        columns.reshape(n_dp * rows, width),
        vecs,
    )


def body(n_mp, n_dp, embeddings, w_in, w_out, means, precisions, log_weight):
    contract_rows = (((0,), (0,)), ((), ()))
    contract_cols = (((1,), (1,)), ((), ()))
    pre = jnp.dot(embeddings, w_in, preferred_element_type=jnp.float32)
    hidden = jax.nn.silu(pre).astype(jnp.bfloat16)
    partial_value = jnp.dot(hidden, w_out, preferred_element_type=jnp.float32)
    spare = jnp.zeros((1, 128), jnp.float32)
    head, hidden_all, emb_cols, _ = exchange(
        partial_value.astype(jnp.bfloat16), hidden, embeddings, spare, n_mp, n_dp, 0
    )
    head_f = head.astype(jnp.float32)
    squares = (head_f * head_f).astype(jnp.bfloat16)
    means_f = means.astype(jnp.float32)
    prec_f = precisions.astype(jnp.float32)
    weighted = (means_f * prec_f).astype(jnp.bfloat16)
    offset = (
        log_weight
        + 0.5 * jnp.sum(jnp.log(prec_f), axis=1)
        - 0.5 * jnp.sum(means_f * means_f * prec_f, axis=1)
    )
    scores = offset[None, :] + lax.dot_general(
        head, weighted, contract_cols, preferred_element_type=jnp.float32
    )
    scores = scores - 0.5 * lax.dot_general(
        squares, precisions, contract_cols, preferred_element_type=jnp.float32
    )
    local_top = jnp.max(scores, axis=1)
    local_total = jnp.sum(jnp.exp(scores - local_top[:, None]), axis=1)
    stats = gather_stats(jnp.stack([local_top, local_total]), n_mp, 1)
    top = jnp.max(stats[:, 0], axis=0)
    total = jnp.sum(stats[:, 1] * jnp.exp(stats[:, 0] - top), axis=0)
    lse = top + jnp.log(total)
    resp = jnp.exp(scores - lse[:, None])
    resp_b = resp.astype(jnp.bfloat16)
    along = jnp.dot(resp_b, precisions, preferred_element_type=jnp.float32)
    shifted = jnp.dot(resp_b, weighted, preferred_element_type=jnp.float32)
    grad_term = head_f * along - shifted
    grad_head, resp_all, head_cols, counts_all = exchange(
        grad_term.astype(jnp.bfloat16),
        resp_b,
        head,
        jnp.sum(resp, axis=0, keepdims=True),
        n_mp,
        n_dp,
        2,
    )
    counts = jnp.sum(counts_all, axis=(0, 1))
    head_cols_f = head_cols.astype(jnp.float32)
    squares_cols = (head_cols_f * head_cols_f).astype(jnp.bfloat16)
    first_moment = lax.dot_general(
        head_cols, resp_all, contract_rows, preferred_element_type=jnp.float32
    )
    second_moment = lax.dot_general(
        squares_cols, resp_all, contract_rows, preferred_element_type=jnp.float32
    )
    back = lax.dot_general(grad_head, w_out, contract_cols, preferred_element_type=jnp.float32)
    sigma = jax.nn.sigmoid(pre)
    grad_pre = (back * sigma * (1.0 + pre * (1.0 - sigma))).astype(jnp.bfloat16)
    embed_term = lax.dot_general(grad_pre, w_in, contract_cols, preferred_element_type=jnp.float32)
    grad_embed, pre_all, grad_cols, _ = exchange(
        embed_term.astype(jnp.bfloat16), grad_pre, grad_head, spare, n_mp, n_dp, 3
    )
    grad_w_in = lax.dot_general(
        emb_cols, pre_all, contract_rows, preferred_element_type=jnp.float32
    ).astype(jnp.bfloat16)
    grad_w_out_t = lax.dot_general(
        grad_cols, hidden_all, contract_rows, preferred_element_type=jnp.float32
    ).astype(jnp.bfloat16)
    return (counts, first_moment, second_moment, grad_w_in, grad_w_out_t, grad_embed)


def solution(mesh):
    return jax.shard_map(
        functools.partial(body, mesh.shape["mp"], mesh.shape["dp"]),
        mesh=mesh,
        in_specs=(
            P(("parts", "dp"), None),
            P(None, "mp"),
            P("mp", None),
            P("mp", None),
            P("mp", None),
            P("mp"),
        ),
        out_specs=(
            P(("parts", "mp")),
            P(("parts", "dp"), "mp"),
            P(("parts", "dp"), "mp"),
            P(("parts", "dp"), "mp"),
            P(("parts", "dp"), "mp"),
            P(("parts", "dp"), None),
        ),
        check_vma=False,
    )
```

time: 289 us -> 143 us (0.49)
  waiting for transfers between devices: 156 us -> 0 us
  Pallas kernels: 0 us -> 105 us
  blocking collectives: 57.7 us -> 0 us
  matrix products: 50.5 us -> 25.2 us
  between operations: 15.8 us -> 0.87 us
  local copies, waits for them, and re-layouts: 1.92 us -> 5.61 us
    all_gather x6 -> x0, waiting for transfers between devices: 112 us -> none  [the longest x1 36.5 us: body(): pre_all = lax.all_gather(grad_pre, 'dp', axis=0, tiled=True)]
    pallas_call x0 -> x4, Pallas kernels: none -> 105 us  [the longest x3 100 us: exchange(): pl.pallas_call(functools.partial(exchange_kernel, n_mp, n_dp, pieces), ou...]
    psum x2 -> x0, blocking collectives: 48.4 us -> none  [the longest x1 40.6 us: body(): head = lax.psum(partial_value, 'mp').astype(jnp.bfloat16)]
    psum x2 -> x0, waiting for transfers between devices: 41.8 us -> none  [the longest x1 41.8 us: body(): grad_head = lax.psum(grad_term.astype(jnp.bfloat16), 'mp')]
    all_gather x1 -> x0, blocking collectives: 9.34 us -> none  [body(): stats = lax.all_gather(jnp.stack([local_top, local_total]), 'mp')]
    unnamed x19 -> x23, local copies, waits for them, and re-layouts: 1.92 us -> 5.61 us
    dot_general x1, matrix products: 4.6 us -> 1.28 us  [body(): lax.dot_general(grad_pre, w_in, contract_cols, preferred_element_type=jnp...]
    dot_general x1, matrix products: 4.62 us -> 1.4 us  [body(): shifted = jnp.dot(resp_b, weighted, preferred_element_type=jnp.float32)]
  transfers between devices with their start and end apart: 8 -> 0, of which waited for: 6 -> 0; matrix products, arithmetic and copies ran while one was open for 10% -> 0% of each run, Pallas kernels for 0% -> 0%
where the time goes in v2:
time: 143 us
  Pallas kernels  105 us (73%)
  matrix products  25.2 us (18%)
  other arithmetic  6.78 us (5%)
  local copies, waits for them, and re-layouts  5.61 us (4%)
    pallas_call x3, Pallas kernels, exchange(): pl.pallas_call(functools.partial(exchange_kernel, n_mp, n_dp, pieces), ou...  100 us
    unnamed x23, local copies, waits for them, and re-layouts  5.61 us
    reduce_sum x1, other arithmetic, body(): jnp.sum(jnp.log(prec_f), axis=1)  5.24 us
    dot_general x1, matrix products, body(): lax.dot_general(grad_head, w_out, contract_cols, preferred_element_type=j...  4.58 us
    pallas_call x1, Pallas kernels, gather_stats(): pl.pallas_call(functools.partial(stats_kernel, n), out_shape=jax.ShapeDty...  4.37 us

profile of v2, /device:TPU:1, one launch (start us, length us, event | category | flops | bytes accessed | tf_op | source)
XLA Modules:
  0.0 143.3 jit_solution(6507092785943264096)
XLA Ops:
  0.6 0.0 copy-start.9
  0.6 0.0 copy-start.4
  0.7 0.0 copy-start.7
  0.7 5.2 %fusion = (f32[2048]{0:T(1024)S(1)}, f32[2048]{0:T(1024)S(1)}) fusion(bf16[2048,1024]{1,0:T(8,128)(2,1)} %param.10, bf16[2048,1024]{1,0:T(8,128)(2,1)} %param.9), kind=kLoop, calls=%fused_computation.4 | loop fusion | flops 12578816 | bytes 8404992 | tf_op jit(solution)/shard_map/reduce_sum | solution.py:223
  5.9 0.0 copy-done.7
  5.9 0.0 copy-done.9
  5.9 0.0 copy-done.4
  6.0 0.0 copy-start.8
  6.0 2.7 %multiply_convert_fusion = (bf16[256,2048]{1,0:T(8,128)(2,1)S(1)}, f32[256,2048]{1,0:T(8,128)}) fusion(bf16[256,1024]{1,0:T(8,128)(2,1)S(1)} %copy-done.4, bf16[1024,2048]{1,0:T(8,128)(2,1)S(1)} %copy-done.9), kind=kOutput, calls=%fused_computation.21 | convolution fusion | flops 1076363264 | bytes 7864320 | tf_op jit(solution)/shard_map/dot_general | solution.py:209
  8.7 0.0 copy-done.8
  8.7 0.0 copy-start.5
  8.7 1.3 convolution_convert_fusion.1
  10.0 0.0 copy-start.6
  10.0 35.8 %shard_map.109 = (bf16[4,64,1024]{2,1,0:T(8,128)(2,1)S(1)}, bf16[4,256,2048]{2,1,0:T(8,128)(2,1)S(1)}, bf16[4,256,256]{2,1,0:T(8,128)(2,1)S(1)}, f32[4,1,128]{2,1,0:T(1,128)}) custom-call(bf16[4,64,1024]{2,1,0:T(8,128)(2,1)S(1)} %bitcast.61, bf16[256,2048]{1,0:T(8,128)(2,1)S(1)} %get-tuple-element.33.block, bf16[256,1024]{1,0:T(8,128)(2,1)S(1)} %copy-done.4, ...), custom_call_target="tpu_custom_call" | custom-call | tf_op jit(solution)/shard_map/pallas_call | solution.py:166
  45.8 0.0 copy-start.2
  45.8 1.9 %copy-done.2 = bf16[4,256,2048]{2,1,0:T(8,128)(2,1)} copy-done((bf16[4,256,2048]{2,1,0:T(8,128)(2,1)}, bf16[4,256,2048]{2,1,0:T(8,128)(2,1)S(1)}, u32[]{:S(2)}) %copy-start.2) | copy-done | bytes 4194328
  47.7 0.0 copy-done.5
  47.7 1.3 convolution_multiply_fusion.1
  49.0 0.0 copy-done.6
  49.0 1.8 %fusion.26 = (f32[256]{0:T(256)S(1)}, f32[256,2048]{1,0:T(8,128)S(1)}) fusion(f32[256,2048]{1,0:T(8,128)S(1)} %convolution_multiply_fusion.1, bf16[256,1024]{1,0:T(8,128)(2,1)S(1)} %bitcast.54, bf16[2048,1024]{1,0:T(8,128)(2,1)S(1)} %copy-done.5, bf16[2048,1024]{1,0:T(8,128)(2,1)S(1)} %copy-done.6, f32[2048]{0:T(1024)S(1)} %multiply_subtract_fusion), kind=kOutput, calls=%fused_computation.44 | convolution fusion | flops 1083703040 | bytes 13116416 | tf_op jit(solution)/shard_map/dot_general | solution.py:226
  50.8 0.4 exponential_reduce_fusion
  51.2 4.4 %shard_map.110 = f32[4,2,256]{2,1,0:T(2,128)S(1)} custom-call(f32[2,256]{1,0:T(2,128)S(1)} %pad_maximum_fusion.in_ref), custom_call_target="tpu_custom_call" | custom-call | tf_op jit(solution)/shard_map/pallas_call | solution.py:58
  55.7 0.4 fusion.8
  56.1 1.3 convolution_multiply_fusion.2
  57.4 1.4 fusion.16
  58.8 32.2 %shard_map.111 = (bf16[4,64,1024]{2,1,0:T(8,128)(2,1)S(1)}, bf16[4,256,2048]{2,1,0:T(8,128)(2,1)S(1)}, bf16[4,256,256]{2,1,0:T(8,128)(2,1)S(1)}, f32[4,1,2048]{2,1,0:T(1,128)S(1)}) custom-call(bf16[4,64,1024]{2,1,0:T(8,128)(2,1)S(1)} %bitcast.57, bf16[256,2048]{1,0:T(8,128)(2,1)S(1)} %get-tuple-element.29.block, bf16[256,1024]{1,0:T(8,128)(2,1)S(1)} %bitcast.56, ...), custom_call_target="tpu_custom_call" | custom-call | tf_op jit(solution)/shard_map/pallas_call | solution.py:166
  91.0 0.0 copy-start
  91.0 2.0 %copy-done = bf16[4,256,2048]{2,1,0:T(8,128)(2,1)} copy-done((bf16[4,256,2048]{2,1,0:T(8,128)(2,1)}, bf16[4,256,2048]{2,1,0:T(8,128)(2,1)S(1)}, u32[]{:S(2)}) %copy-start) | copy-done | bytes 4194328
  93.0 0.6 reduce_sum.59
  93.6 0.0 copy-start.10
  93.6 4.6 %fusion.7.block = bf16[256,2048]{1,0:T(8,128)(2,1)S(1)} fusion(bf16[256,1024]{1,0:T(8,128)(2,1)S(1)} %bitcast.58, bf16[2048,1024]{1,0:T(8,128)(2,1)} %param.8, f32[256,2048]{1,0:T(8,128)} %get-tuple-element.34), kind=kOutput, calls=%fused_computation.18 | convolution fusion | flops 1078460416 | bytes 7864320 | tf_op jit(solution)/shard_map/dot_general | solution.py:261
  98.2 0.0 copy-done.10
  98.2 0.0 copy-start.1
  98.2 1.3 convolution_convert_fusion
  99.5 0.9 copy-done.1
  100.4 2.6 %convolution_bitcast_fusion.2 = f32[256,2048]{1,0:T(8,128)} fusion(bf16[4,256,2048]{2,1,0:T(8,128)(2,1)S(1)} %copy-done.1, bf16[4,256,256]{2,1,0:T(8,128)(2,1)S(1)} %get-tuple-element.18), kind=kOutput, calls=%fused_computation.12 | convolution fusion | flops 1074528256 | bytes 6815744 | tf_op jit(solution)/shard_map/dot_general | solution.py:258
  103.0 0.0 copy-start.3
  103.0 2.6 %convolution_bitcast_fusion.3 = f32[256,2048]{1,0:T(8,128)} fusion(bf16[4,256,256]{2,1,0:T(8,128)(2,1)S(1)} %get-tuple-element.18, bf16[4,256,2048]{2,1,0:T(8,128)(2,1)S(1)} %copy-done.1), kind=kOutput, calls=%fused_computation.13 | convolution fusion | flops 1073741824 | bytes 6815744 | tf_op jit(solution)/shard_map/dot_general | solution.py:255
  105.6 32.4 %shard_map.112 = (bf16[4,64,1024]{2,1,0:T(8,128)(2,1)S(1)}, bf16[4,256,2048]{2,1,0:T(8,128)(2,1)S(1)}, bf16[4,256,256]{2,1,0:T(8,128)(2,1)S(1)}, f32[4,1,128]{2,1,0:T(1,128)}) custom-call(bf16[4,64,1024]{2,1,0:T(8,128)(2,1)S(1)} %bitcast.60, bf16[256,2048]{1,0:T(8,128)(2,1)S(1)} %fusion.7.block, bf16[256,1024]{1,0:T(8,128)(2,1)S(1)} %bitcast.59, ...), custom_call_target="tpu_custom_call" | custom-call | tf_op jit(solution)/shard_map/pallas_call | solution.py:166
  138.0 0.0 copy-done.3
  138.0 2.2 %fusion.6 = bf16[256,2048]{1,0:T(8,128)(2,1)} fusion(bf16[4,256,256]{2,1,0:T(8,128)(2,1)S(1)} %get-tuple-element.23, bf16[4,256,2048]{2,1,0:T(8,128)(2,1)S(1)} %copy-done.3), kind=kOutput, calls=%fused_computation.17 | convolution fusion | flops 1074266112 | bytes 5767168 | tf_op jit(solution)/shard_map/dot_general | solution.py:271
  140.3 2.2 %fusion.5 = bf16[256,2048]{1,0:T(8,128)(2,1)} fusion(bf16[4,256,256]{2,1,0:T(8,128)(2,1)S(1)} %get-tuple-element.20, bf16[4,256,2048]{2,1,0:T(8,128)(2,1)S(1)} %get-tuple-element.22), kind=kOutput, calls=%fused_computation.16 | convolution fusion | flops 1074266112 | bytes 5767168 | tf_op jit(solution)/shard_map/dot_general | solution.py:268
  142.5 0.8 copy.35
  (6 shorter events, 0.1 us)
Async XLA Ops:
  0.6 5.3 %copy-start.9 = (bf16[1024,2048]{1,0:T(8,128)(2,1)S(1)}, bf16[1024,2048]{1,0:T(8,128)(2,1)}, u32[]{:S(2)}) copy-start(bf16[1024,2048]{1,0:T(8,128)(2,1)} %param.7) | copy-start | bytes 12582916
  0.6 5.3 %copy-start.4 = (bf16[256,1024]{1,0:T(8,128)(2,1)S(1)}, bf16[256,1024]{1,0:T(8,128)(2,1)}, u32[]{:S(2)}) copy-start(bf16[256,1024]{1,0:T(8,128)(2,1)} %wide.1) | copy-start | bytes 1572868
  0.7 5.3 %copy-start.7 = (f32[2048]{0:T(1024)S(1)}, f32[2048]{0:T(1024)}, u32[]{:S(2)}) copy-start(f32[2048]{0:T(1024)} %param.11) | copy-start | bytes 24580
  6.0 2.7 %copy-start.8 = (bf16[2048,1024]{1,0:T(8,128)(2,1)S(1)}, bf16[2048,1024]{1,0:T(8,128)(2,1)}, u32[]{:S(2)}) copy-start(bf16[2048,1024]{1,0:T(8,128)(2,1)} %param.8) | copy-start | bytes 12582916
  8.7 39.0 %copy-start.5 = (bf16[2048,1024]{1,0:T(8,128)(2,1)S(1)}, bf16[2048,1024]{1,0:T(8,128)(2,1)}, u32[]{:S(2)}) copy-start(bf16[2048,1024]{1,0:T(8,128)(2,1)} %param.10) | copy-start | bytes 12582916
  10.0 39.0 %copy-start.6 = (bf16[2048,1024]{1,0:T(8,128)(2,1)S(1)}, bf16[2048,1024]{1,0:T(8,128)(2,1)}, u32[]{:S(2)}) copy-start(bf16[2048,1024]{1,0:T(8,128)(2,1)} %param.9) | copy-start | bytes 12582916
  45.8 1.9 %copy-start.2 = (bf16[4,256,2048]{2,1,0:T(8,128)(2,1)}, bf16[4,256,2048]{2,1,0:T(8,128)(2,1)S(1)}, u32[]{:S(2)}) copy-start(bf16[4,256,2048]{2,1,0:T(8,128)(2,1)S(1)} %get-tuple-element.24) | copy-start | bytes 12582916
  91.0 2.0 %copy-start = (bf16[4,256,2048]{2,1,0:T(8,128)(2,1)}, bf16[4,256,2048]{2,1,0:T(8,128)(2,1)S(1)}, u32[]{:S(2)}) copy-start(bf16[4,256,2048]{2,1,0:T(8,128)(2,1)S(1)} %get-tuple-element.19) | copy-start | bytes 12582916
  93.6 4.6 %copy-start.10 = (bf16[1024,2048]{1,0:T(8,128)(2,1)S(1)}, bf16[1024,2048]{1,0:T(8,128)(2,1)}, u32[]{:S(2)}) copy-start(bf16[1024,2048]{1,0:T(8,128)(2,1)} %param.7) | copy-start | bytes 12582916
  98.2 2.2 %copy-start.1 = (bf16[4,256,2048]{2,1,0:T(8,128)(2,1)S(1)}, bf16[4,256,2048]{2,1,0:T(8,128)(2,1)}, u32[]{:S(2)}) copy-start(bf16[4,256,2048]{2,1,0:T(8,128)(2,1)} %copy-done) | copy-start | bytes 12582916
  103.0 35.0 %copy-start.3 = (bf16[4,256,2048]{2,1,0:T(8,128)(2,1)S(1)}, bf16[4,256,2048]{2,1,0:T(8,128)(2,1)}, u32[]{:S(2)}) copy-start(bf16[4,256,2048]{2,1,0:T(8,128)(2,1)} %copy-done.2) | copy-start | bytes 12582916

commit v3 on v2

--- a/solution.py
+++ b/solution.py
@@ -1,4 +1,5 @@
 import functools
+import math
 
 import jax
 import jax.numpy as jnp
@@ -67,10 +68,45 @@
     )(stats)
 
 
-def exchange_kernel(n_mp, n_dp, pieces, term, block, wide, vec, *refs):
-    (total, gathered, columns, vecs, landed) = refs[:5]
-    (sum_s, sum_r, out_s, out_r, col_s, col_r, vec_s, vec_r) = refs[5:13]
-    (pair_s, pair_r, far_s, far_r, fwd_s, fwd_r, own_sem) = refs[13:]
+def offset_side(means, precisions, out):
+    tile = math.gcd(means.shape[0], 64)
+    depth = means.shape[1]
+    lanes = out.shape[1]
+
+    def step(i, carry):
+        rows = pl.ds(pl.multiple_of(i * tile, tile), tile)
+        acc = jnp.zeros((tile, lanes), jnp.float32)
+        for col in range(0, depth, lanes):
+            mean = means[rows, col : col + lanes].astype(jnp.float32)
+            prec = precisions[rows, col : col + lanes].astype(jnp.float32)
+            acc = acc + (jnp.log(prec) - mean * mean * prec)
+        out[rows, :] = 0.5 * acc
+        return carry
+
+    lax.fori_loop(0, means.shape[0] // tile, step, 0)
+
+
+def moment_side(feats, resp, first, second):
+    tile = math.gcd(resp.shape[1], 256)
+    half = first.shape[0]
+
+    def step(i, carry):
+        cols = pl.ds(pl.multiple_of(i * tile, tile), tile)
+        value = jnp.dot(feats[...], resp[:, cols], preferred_element_type=jnp.float32)
+        first[:, cols] = value[:half]
+        second[:, cols] = value[half:]
+        return carry
+
+    lax.fori_loop(0, resp.shape[1] // tile, step, 0)
+
+
+def exchange_kernel(n_mp, n_dp, pieces, side, n_in, n_out, term, block, wide, vec, *refs):
+    side_in, refs = refs[:n_in], refs[n_in:]
+    (total, gathered, columns, vecs), refs = refs[:4], refs[4:]
+    side_out, refs = refs[:n_out], refs[n_out:]
+    landed = refs[0]
+    (sum_s, sum_r, out_s, out_r, col_s, col_r, vec_s, vec_r) = refs[1:9]
+    (pair_s, pair_r, far_s, far_r, fwd_s, fwd_r, own_sem) = refs[9:]
     greet((("mp", n_mp), ("dp", n_dp)))
     me, dp = lax.axis_index("mp"), lax.axis_index("dp")
     n_x = n_dp // 2
@@ -119,6 +155,9 @@
     for copy in own:
         copy.start()
 
+    if side is not None:
+        side(*side_in, *side_out)
+
     acc = term[me].astype(jnp.float32)
     for step in range(1, n_mp):
         peer = lax.rem(me + step, n_mp)
@@ -157,22 +196,23 @@
         copy.wait_send()
 
 
-def exchange(term, block, wide, vec, n_mp, n_dp, collective_id):
+def exchange(term, block, wide, vec, n_mp, n_dp, collective_id, side=None, side_in=(), side_out=()):
     pieces = 4 if block.shape[0] % 64 == 0 else 1
     rows, width = wide.shape[0], wide.shape[1] // n_dp
     dma = pltpu.SemaphoreType.DMA
     chunk = (n_mp, term.shape[0] // n_mp, term.shape[1])
     vmem = pl.BlockSpec(memory_space=pltpu.VMEM)
-    total, gathered, columns, vecs = pl.pallas_call(
-        functools.partial(exchange_kernel, n_mp, n_dp, pieces),
+    total, gathered, columns, vecs, *extra = pl.pallas_call(
+        functools.partial(exchange_kernel, n_mp, n_dp, pieces, side, len(side_in), len(side_out)),
         out_shape=(
             jax.ShapeDtypeStruct(chunk, term.dtype),
             jax.ShapeDtypeStruct((n_dp,) + block.shape, block.dtype),
             jax.ShapeDtypeStruct((n_dp, rows, width), wide.dtype),
             jax.ShapeDtypeStruct((n_dp,) + vec.shape, vec.dtype),
-        ),
-        in_specs=[vmem] * 4,
-        out_specs=(vmem,) * 4,
+        )
+        + tuple(side_out),
+        in_specs=[vmem] * (4 + len(side_in)),
+        out_specs=(vmem,) * (4 + len(side_out)),
         scratch_shapes=[
             pltpu.VMEM(chunk, term.dtype),
             dma((n_mp,)),
@@ -192,14 +232,15 @@
             dma((3,)),
         ],
         compiler_params=pltpu.CompilerParams(
-            collective_id=collective_id, has_side_effects=True, vmem_limit_bytes=20 << 20
+            collective_id=collective_id, has_side_effects=True, vmem_limit_bytes=32 << 20
         ),
-    )(term.reshape(chunk), block, wide, vec)
+    )(term.reshape(chunk), block, wide, vec, *side_in)
     return (
         total.reshape(term.shape),
         gathered.reshape(n_dp * block.shape[0], block.shape[1]),
         columns.reshape(n_dp * rows, width),
         vecs,
+        *extra,
     )
 
 
@@ -210,19 +251,24 @@
     hidden = jax.nn.silu(pre).astype(jnp.bfloat16)
     partial_value = jnp.dot(hidden, w_out, preferred_element_type=jnp.float32)
     spare = jnp.zeros((1, 128), jnp.float32)
-    head, hidden_all, emb_cols, _ = exchange(
-        partial_value.astype(jnp.bfloat16), hidden, embeddings, spare, n_mp, n_dp, 0
+    head, hidden_all, emb_cols, _, halves = exchange(
+        partial_value.astype(jnp.bfloat16),
+        hidden,
+        embeddings,
+        spare,
+        n_mp,
+        n_dp,
+        0,
+        offset_side,
+        (means, precisions),
+        (jax.ShapeDtypeStruct((means.shape[0], 128), jnp.float32),),
     )
     head_f = head.astype(jnp.float32)
     squares = (head_f * head_f).astype(jnp.bfloat16)
     means_f = means.astype(jnp.float32)
     prec_f = precisions.astype(jnp.float32)
     weighted = (means_f * prec_f).astype(jnp.bfloat16)
-    offset = (
-        log_weight
-        + 0.5 * jnp.sum(jnp.log(prec_f), axis=1)
-        - 0.5 * jnp.sum(means_f * means_f * prec_f, axis=1)
-    )
+    offset = log_weight + jnp.sum(halves, axis=1)
     scores = offset[None, :] + lax.dot_general(
         head, weighted, contract_cols, preferred_element_type=jnp.float32
     )
@@ -252,18 +298,23 @@
     counts = jnp.sum(counts_all, axis=(0, 1))
     head_cols_f = head_cols.astype(jnp.float32)
     squares_cols = (head_cols_f * head_cols_f).astype(jnp.bfloat16)
-    first_moment = lax.dot_general(
-        head_cols, resp_all, contract_rows, preferred_element_type=jnp.float32
-    )
-    second_moment = lax.dot_general(
-        squares_cols, resp_all, contract_rows, preferred_element_type=jnp.float32
-    )
+    feats = jnp.concatenate([head_cols, squares_cols], axis=1).T
+    moment = jax.ShapeDtypeStruct((head_cols.shape[1], resp_all.shape[1]), jnp.float32)
     back = lax.dot_general(grad_head, w_out, contract_cols, preferred_element_type=jnp.float32)
     sigma = jax.nn.sigmoid(pre)
     grad_pre = (back * sigma * (1.0 + pre * (1.0 - sigma))).astype(jnp.bfloat16)
     embed_term = lax.dot_general(grad_pre, w_in, contract_cols, preferred_element_type=jnp.float32)
-    grad_embed, pre_all, grad_cols, _ = exchange(
-        embed_term.astype(jnp.bfloat16), grad_pre, grad_head, spare, n_mp, n_dp, 3
+    grad_embed, pre_all, grad_cols, _, first_moment, second_moment = exchange(
+        embed_term.astype(jnp.bfloat16),
+        grad_pre,
+        grad_head,
+        spare,
+        n_mp,
+        n_dp,
+        3,
+        moment_side,
+        (feats, resp_all),
+        (moment, moment),
     )
     grad_w_in = lax.dot_general(
         emb_cols, pre_all, contract_rows, preferred_element_type=jnp.float32

time: 143 us -> 146 us (1.021)
  other arithmetic: 6.78 us -> 2.04 us
  matrix products: 25.2 us -> 29.1 us
  local copies, waits for them, and re-layouts: 5.61 us -> 9.47 us
    dot_general x2 -> x0, matrix products: 5.19 us -> none  [the longest x1 2.6 us: body(): lax.dot_general(squares_cols, resp_all, contract_rows, preferred_element_...]
    reduce_sum x1, other arithmetic: 5.24 us -> 0.34 us  [body(): offset = log_weight + jnp.sum(halves, axis=1)]
    unnamed x23 -> x25, local copies, waits for them, and re-layouts: 5.61 us -> 9.26 us
    dot_general x1, matrix products: 2.7 us -> 5.11 us  [body(): pre = jnp.dot(embeddings, w_in, preferred_element_type=jnp.float32)]
    dot_general x1, matrix products: 1.28 us -> 3.63 us  [body(): lax.dot_general(squares, precisions, contract_cols, preferred_element_typ...]
    dot_general x1, matrix products: 1.28 us -> 3.62 us  [body(): lax.dot_general(grad_pre, w_in, contract_cols, preferred_element_type=jnp...]
    dot_general x1, matrix products: 1.77 us -> 3.79 us  [body(): lax.dot_general(head, weighted, contract_cols, preferred_element_type=jnp...]
where the time goes in v3:
time: 146 us
  Pallas kernels  105 us (72%)
  matrix products  29.1 us (20%)
  local copies, waits for them, and re-layouts  9.47 us (6%)
  other arithmetic  2.04 us (1%)
    pallas_call x3, Pallas kernels, exchange(): pl.pallas_call(functools.partial(exchange_kernel, n_mp, n_dp, pieces, sid...  100 us
    unnamed x25, local copies, waits for them, and re-layouts  9.26 us
    dot_general x1, matrix products, body(): pre = jnp.dot(embeddings, w_in, preferred_element_type=jnp.float32)  5.11 us
    dot_general x1, matrix products, body(): lax.dot_general(grad_head, w_out, contract_cols, preferred_element_type=j...  4.4 us
    pallas_call x1, Pallas kernels, gather_stats(): pl.pallas_call(functools.partial(stats_kernel, n), out_shape=jax.ShapeDty...  4.37 us
    dot_general x1, matrix products, body(): lax.dot_general(head, weighted, contract_cols, preferred_element_type=jnp...  3.79 us
    dot_general x1, matrix products, body(): lax.dot_general(squares, precisions, contract_cols, preferred_element_typ...  3.63 us
    dot_general x1, matrix products, body(): lax.dot_general(grad_pre, w_in, contract_cols, preferred_element_type=jnp...  3.62 us

profile of v3, /device:TPU:1, one launch (start us, length us, event | category | flops | bytes accessed | tf_op | source)
XLA Modules:
  0.0 146.2 jit_solution(8106007076205197206)
XLA Ops:
  0.6 0.0 copy-start.10
  0.6 0.0 copy-start.2
  0.7 5.1 %multiply_convert_fusion.1 = (bf16[256,2048]{1,0:T(8,128)(2,1)S(1)}, f32[256,2048]{1,0:T(8,128)}) fusion(bf16[256,1024]{1,0:T(8,128)(2,1)} %wide.1, bf16[1024,2048]{1,0:T(8,128)(2,1)} %param.7), kind=kOutput, calls=%fused_computation.13 | convolution fusion | flops 1076363264 | bytes 7864320 | tf_op jit(solution)/shard_map/dot_general | solution.py:250
  5.8 0.0 copy-start
  5.8 0.0 copy-start.8
  5.8 0.0 copy-done.10
  5.8 1.3 convolution_convert_fusion.1
  7.1 0.0 copy-done.2
  7.1 0.9 copy-done
  8.0 0.1 copy-done.8
  8.1 0.0 copy-start.9
  8.1 35.8 %shard_map.109 = (bf16[4,64,1024]{2,1,0:T(8,128)(2,1)S(1)}, bf16[4,256,2048]{2,1,0:T(8,128)(2,1)S(1)}, bf16[4,256,256]{2,1,0:T(8,128)(2,1)S(1)}, f32[4,1,128]{2,1,0:T(1,128)}, f32[2048,128]{1,0:T(8,128)S(1)}) custom-call(bf16[4,64,1024]{2,1,0:T(8,128)(2,1)S(1)} %bitcast.61, bf16[256,2048]{1,0:T(8,128)(2,1)S(1)} %get-tuple-element.37.block, ...), custom_call_target="tpu_custom_call" | custom-call | tf_op jit(solution)/shard_map/pallas_call | solution.py:205
  43.8 0.0 copy-start.4
  43.8 1.9 %copy-done.4 = bf16[4,256,2048]{2,1,0:T(8,128)(2,1)} copy-done((bf16[4,256,2048]{2,1,0:T(8,128)(2,1)}, bf16[4,256,2048]{2,1,0:T(8,128)(2,1)S(1)}, u32[]{:S(2)}) %copy-start.4) | copy-done | bytes 4194328
  45.8 0.3 reduce_sum.45
  46.1 0.0 copy-done.9
  46.1 0.0 copy-start.1
  46.1 3.6 %convolution_multiply_fusion.1 = f32[256,2048]{1,0:T(8,128)S(1)} fusion(bf16[2048,1024]{1,0:T(8,128)(2,1)} %refs_1_.1, bf16[256,1024]{1,0:T(8,128)(2,1)S(1)} %bitcast.51), kind=kOutput, calls=%fused_computation.2 | convolution fusion | flops 1075052544 | bytes 6815744 | tf_op jit(solution)/shard_map/dot_general | solution.py:275
  49.8 0.0 copy-done.1
  49.8 3.8 %fusion.17 = (f32[256]{0:T(256)S(1)}, f32[256,2048]{1,0:T(8,128)S(1)}) fusion(f32[256,2048]{1,0:T(8,128)S(1)} %convolution_multiply_fusion.1, bf16[256,1024]{1,0:T(8,128)(2,1)S(1)} %bitcast.52, bf16[2048,1024]{1,0:T(8,128)(2,1)S(1)} %copy-done.1, bf16[2048,1024]{1,0:T(8,128)(2,1)} %refs_0_.1, f32[2048]{0:T(1024)S(1)} %add.27), kind=kOutput, calls=%fused_computation.36 | convolution fusion | flops 1083703040 | bytes 13116416 | tf_op jit(solution)/shard_map/dot_general | solution.py:272
  53.6 0.4 exponential_reduce_fusion
  54.0 4.4 %shard_map.110 = f32[4,2,256]{2,1,0:T(2,128)S(1)} custom-call(f32[2,256]{1,0:T(2,128)S(1)} %pad_maximum_fusion.in_ref), custom_call_target="tpu_custom_call" | custom-call | tf_op jit(solution)/shard_map/pallas_call | solution.py:59
  58.5 0.4 fusion.5
  58.9 0.0 copy-start.3
  58.9 1.3 convolution_multiply_fusion.2
  60.1 0.9 copy-done.3
  61.1 1.5 %fusion.9 = bf16[256,1024]{1,0:T(8,128)(2,1)S(1)} fusion(f32[256,1024]{1,0:T(8,128)S(1)} %convolution_multiply_fusion.2, bf16[256,2048]{1,0:T(8,128)(2,1)S(1)} %get-tuple-element.33.block, bf16[2048,1024]{1,0:T(8,128)(2,1)S(1)} %copy-done.1, bf16[2048,1024]{1,0:T(8,128)(2,1)S(1)} %copy-done.3), kind=kOutput, calls=%fused_computation.21 | convolution fusion | flops 1082654720 | bytes 11010048 | tf_op jit(solution)/shard_map/dot_general | solution.py:287
  62.6 32.1 %shard_map.111 = (bf16[4,64,1024]{2,1,0:T(8,128)(2,1)S(1)}, bf16[4,256,2048]{2,1,0:T(8,128)(2,1)S(1)}, bf16[4,256,256]{2,1,0:T(8,128)(2,1)S(1)}, f32[4,1,2048]{2,1,0:T(1,128)S(1)}) custom-call(bf16[4,64,1024]{2,1,0:T(8,128)(2,1)S(1)} %bitcast.55, bf16[256,2048]{1,0:T(8,128)(2,1)S(1)} %get-tuple-element.33.block, bf16[256,1024]{1,0:T(8,128)(2,1)S(1)} %bitcast.54, ...), custom_call_target="tpu_custom_call" | custom-call | tf_op jit(solution)/shard_map/pallas_call | solution.py:205
  94.7 0.0 copy-start.6
  94.7 2.0 %copy-done.6 = bf16[4,256,2048]{2,1,0:T(8,128)(2,1)} copy-done((bf16[4,256,2048]{2,1,0:T(8,128)(2,1)}, bf16[4,256,2048]{2,1,0:T(8,128)(2,1)S(1)}, u32[]{:S(2)}) %copy-start.6) | copy-done | bytes 4194328
  96.7 0.6 reduce_sum.49
  97.3 4.4 %fusion.4.block = bf16[256,2048]{1,0:T(8,128)(2,1)S(1)} fusion(bf16[256,1024]{1,0:T(8,128)(2,1)S(1)} %bitcast.58, bf16[2048,1024]{1,0:T(8,128)(2,1)} %param.8, f32[256,2048]{1,0:T(8,128)} %get-tuple-element.38), kind=kOutput, calls=%fused_computation.10 | convolution fusion | flops 1078460416 | bytes 7864320 | tf_op jit(solution)/shard_map/dot_general | solution.py:303
  101.7 0.2 copy.18
  102.0 0.1 multiply_convert_fusion.8
  102.1 0.1 maximum_bitcast_fusion.refs_0_
  102.1 0.0 copy-start.7
  102.2 3.6 %convolution_convert_fusion = bf16[256,1024]{1,0:T(8,128)(2,1)S(1)} fusion(bf16[256,2048]{1,0:T(8,128)(2,1)S(1)} %fusion.4.block, bf16[1024,2048]{1,0:T(8,128)(2,1)} %param.7), kind=kOutput, calls=%fused_computation.22 | convolution fusion | flops 1074003968 | bytes 5767168 | tf_op jit(solution)/shard_map/dot_general | solution.py:306
  105.8 0.0 copy-start.5
  105.8 0.0 copy-done.7
  105.8 32.5 %shard_map.112 = (bf16[4,64,1024]{2,1,0:T(8,128)(2,1)S(1)}, bf16[4,256,2048]{2,1,0:T(8,128)(2,1)S(1)}, bf16[4,256,256]{2,1,0:T(8,128)(2,1)S(1)}, f32[4,1,128]{2,...) custom-call(bf16[4,64,1024]{2,1,0:T(8,128)(2,1)S(1)} %bitcast.60, bf16[256,2048]{1,0:T(8,128)(2,1)S(1)} %fusion.4.block, ...), custom_call_target="tpu_custom_call" | custom-call | tf_op jit(solution)/shard_map/pallas_call | solution.py:205
  138.3 0.0 copy-done.5
  138.3 2.2 %fusion.3 = bf16[256,2048]{1,0:T(8,128)(2,1)} fusion(bf16[4,256,256]{2,1,0:T(8,128)(2,1)S(1)} %get-tuple-element.29, bf16[4,256,2048]{2,1,0:T(8,128)(2,1)S(1)} %copy-done.5), kind=kOutput, calls=%fused_computation.9 | convolution fusion | flops 1074266112 | bytes 5767168 | tf_op jit(solution)/shard_map/dot_general | solution.py:322
  140.6 2.2 %fusion.2 = bf16[256,2048]{1,0:T(8,128)(2,1)} fusion(bf16[4,256,256]{2,1,0:T(8,128)(2,1)S(1)} %get-tuple-element.27, bf16[4,256,2048]{2,1,0:T(8,128)(2,1)S(1)} %get-tuple-element.28), kind=kOutput, calls=%fused_computation.8 | convolution fusion | flops 1074266112 | bytes 5767168 | tf_op jit(solution)/shard_map/dot_general | solution.py:319
  142.8 1.3 copy.35
  144.1 1.3 copy.36
  145.5 0.8 copy.37
  (6 shorter events, 0.1 us)
Async XLA Ops:
  0.6 5.1 %copy-start.10 = (bf16[2048,1024]{1,0:T(8,128)(2,1)S(1)}, bf16[2048,1024]{1,0:T(8,128)(2,1)}, u32[]{:S(2)}) copy-start(bf16[2048,1024]{1,0:T(8,128)(2,1)} %param.8) | copy-start | bytes 12582916
  0.6 6.4 %copy-start.2 = (bf16[2048,1024]{1,0:T(8,128)(2,1)S(1)}, bf16[2048,1024]{1,0:T(8,128)(2,1)}, u32[]{:S(2)}) copy-start(bf16[2048,1024]{1,0:T(8,128)(2,1)} %refs_0_.1) | copy-start | bytes 12582916
  5.8 2.2 %copy-start = (bf16[2048,1024]{1,0:T(8,128)(2,1)S(1)}, bf16[2048,1024]{1,0:T(8,128)(2,1)}, u32[]{:S(2)}) copy-start(bf16[2048,1024]{1,0:T(8,128)(2,1)} %refs_1_.1) | copy-start | bytes 12582916
  5.8 2.3 %copy-start.8 = (bf16[256,1024]{1,0:T(8,128)(2,1)S(1)}, bf16[256,1024]{1,0:T(8,128)(2,1)}, u32[]{:S(2)}) copy-start(bf16[256,1024]{1,0:T(8,128)(2,1)} %wide.1) | copy-start | bytes 1572868
  8.1 38.0 %copy-start.9 = (f32[2048]{0:T(1024)S(1)}, f32[2048]{0:T(1024)}, u32[]{:S(2)}) copy-start(f32[2048]{0:T(1024)} %param.11) | copy-start | bytes 24580
  43.8 1.9 %copy-start.4 = (bf16[4,256,2048]{2,1,0:T(8,128)(2,1)}, bf16[4,256,2048]{2,1,0:T(8,128)(2,1)S(1)}, u32[]{:S(2)}) copy-start(bf16[4,256,2048]{2,1,0:T(8,128)(2,1)S(1)} %get-tuple-element.30) | copy-start | bytes 12582916
  46.1 3.7 %copy-start.1 = (bf16[2048,1024]{1,0:T(8,128)(2,1)S(1)}, bf16[2048,1024]{1,0:T(8,128)(2,1)}, u32[]{:S(2)}) copy-start(bf16[2048,1024]{1,0:T(8,128)(2,1)} %refs_1_.1) | copy-start | bytes 12582916
  58.9 2.2 %copy-start.3 = (bf16[2048,1024]{1,0:T(8,128)(2,1)S(1)}, bf16[2048,1024]{1,0:T(8,128)(2,1)}, u32[]{:S(2)}) copy-start(bf16[2048,1024]{1,0:T(8,128)(2,1)} %refs_0_.1) | copy-start | bytes 12582916
  94.7 2.0 %copy-start.6 = (bf16[4,256,2048]{2,1,0:T(8,128)(2,1)}, bf16[4,256,2048]{2,1,0:T(8,128)(2,1)S(1)}, u32[]{:S(2)}) copy-start(bf16[4,256,2048]{2,1,0:T(8,128)(2,1)S(1)} %get-tuple-element.24) | copy-start | bytes 12582916
  102.1 3.7 %copy-start.7 = (bf16[4,256,2048]{2,1,0:T(8,128)(2,1)S(1)}, bf16[4,256,2048]{2,1,0:T(8,128)(2,1)}, u32[]{:S(2)}) copy-start(bf16[4,256,2048]{2,1,0:T(8,128)(2,1)} %copy-done.6) | copy-start | bytes 12582916
  105.8 32.5 %copy-start.5 = (bf16[4,256,2048]{2,1,0:T(8,128)(2,1)S(1)}, bf16[4,256,2048]{2,1,0:T(8,128)(2,1)}, u32[]{:S(2)}) copy-start(bf16[4,256,2048]{2,1,0:T(8,128)(2,1)} %copy-done.4) | copy-start | bytes 12582916

commit v4 on v2

--- a/solution.py
+++ b/solution.py
@@ -158,7 +158,7 @@
 
 
 def exchange(term, block, wide, vec, n_mp, n_dp, collective_id):
-    pieces = 4 if block.shape[0] % 64 == 0 else 1
+    pieces = 2 if block.shape[0] % 32 == 0 else 1
     rows, width = wide.shape[0], wide.shape[1] // n_dp
     dma = pltpu.SemaphoreType.DMA
     chunk = (n_mp, term.shape[0] // n_mp, term.shape[1])

time: 143 us -> 143 us (level)
  no operation moved by 1% of the time
where the time goes in v4:
time: 143 us
  Pallas kernels  104 us (73%)
  matrix products  25.2 us (18%)
  other arithmetic  6.78 us (5%)
  local copies, waits for them, and re-layouts  5.61 us (4%)
    pallas_call x3, Pallas kernels, exchange(): pl.pallas_call(functools.partial(exchange_kernel, n_mp, n_dp, pieces), ou...  100 us
    unnamed x23, local copies, waits for them, and re-layouts  5.61 us
    reduce_sum x1, other arithmetic, body(): jnp.sum(jnp.log(prec_f), axis=1)  5.24 us
    dot_general x1, matrix products, body(): lax.dot_general(grad_head, w_out, contract_cols, preferred_element_type=j...  4.58 us
    pallas_call x1, Pallas kernels, gather_stats(): pl.pallas_call(functools.partial(stats_kernel, n), out_shape=jax.ShapeDty...  4.37 us

profile of v4, /device:TPU:1, one launch (start us, length us, event | category | flops | bytes accessed | tf_op | source)
XLA Modules:
  0.0 142.9 jit_solution(18394780537072539332)
XLA Ops:
  0.6 0.0 copy-start.9
  0.6 0.0 copy-start.4
  0.7 0.0 copy-start.7
  0.7 5.2 %fusion = (f32[2048]{0:T(1024)S(1)}, f32[2048]{0:T(1024)S(1)}) fusion(bf16[2048,1024]{1,0:T(8,128)(2,1)} %param.10, bf16[2048,1024]{1,0:T(8,128)(2,1)} %param.9), kind=kLoop, calls=%fused_computation.4 | loop fusion | flops 12578816 | bytes 8404992 | tf_op jit(solution)/shard_map/reduce_sum | solution.py:223
  5.9 0.0 copy-done.7
  5.9 0.0 copy-done.9
  5.9 0.0 copy-done.4
  6.0 0.0 copy-start.8
  6.0 2.7 %multiply_convert_fusion = (bf16[256,2048]{1,0:T(8,128)(2,1)S(1)}, f32[256,2048]{1,0:T(8,128)}) fusion(bf16[256,1024]{1,0:T(8,128)(2,1)S(1)} %copy-done.4, bf16[1024,2048]{1,0:T(8,128)(2,1)S(1)} %copy-done.9), kind=kOutput, calls=%fused_computation.21 | convolution fusion | flops 1076363264 | bytes 7864320 | tf_op jit(solution)/shard_map/dot_general | solution.py:209
  8.7 0.0 copy-done.8
  8.7 0.0 copy-start.5
  8.7 1.3 convolution_convert_fusion.1
  10.0 0.0 copy-start.6
  10.0 35.6 %shard_map.109 = (bf16[4,64,1024]{2,1,0:T(8,128)(2,1)S(1)}, bf16[4,256,2048]{2,1,0:T(8,128)(2,1)S(1)}, bf16[4,256,256]{2,1,0:T(8,128)(2,1)S(1)}, f32[4,1,128]{2,1,0:T(1,128)}) custom-call(bf16[4,64,1024]{2,1,0:T(8,128)(2,1)S(1)} %bitcast.61, bf16[256,2048]{1,0:T(8,128)(2,1)S(1)} %get-tuple-element.33.block, bf16[256,1024]{1,0:T(8,128)(2,1)S(1)} %copy-done.4, ...), custom_call_target="tpu_custom_call" | custom-call | tf_op jit(solution)/shard_map/pallas_call | solution.py:166
  45.6 0.0 copy-start.2
  45.6 1.9 %copy-done.2 = bf16[4,256,2048]{2,1,0:T(8,128)(2,1)} copy-done((bf16[4,256,2048]{2,1,0:T(8,128)(2,1)}, bf16[4,256,2048]{2,1,0:T(8,128)(2,1)S(1)}, u32[]{:S(2)}) %copy-start.2) | copy-done | bytes 4194328
  47.6 0.0 copy-done.5
  47.6 1.3 convolution_multiply_fusion.1
  48.8 0.0 copy-done.6
  48.9 1.8 %fusion.26 = (f32[256]{0:T(256)S(1)}, f32[256,2048]{1,0:T(8,128)S(1)}) fusion(f32[256,2048]{1,0:T(8,128)S(1)} %convolution_multiply_fusion.1, bf16[256,1024]{1,0:T(8,128)(2,1)S(1)} %bitcast.54, bf16[2048,1024]{1,0:T(8,128)(2,1)S(1)} %copy-done.5, bf16[2048,1024]{1,0:T(8,128)(2,1)S(1)} %copy-done.6, f32[2048]{0:T(1024)S(1)} %multiply_subtract_fusion), kind=kOutput, calls=%fused_computation.44 | convolution fusion | flops 1083703040 | bytes 13116416 | tf_op jit(solution)/shard_map/dot_general | solution.py:226
  50.6 0.4 exponential_reduce_fusion
  51.1 4.4 %shard_map.110 = f32[4,2,256]{2,1,0:T(2,128)S(1)} custom-call(f32[2,256]{1,0:T(2,128)S(1)} %pad_maximum_fusion.in_ref), custom_call_target="tpu_custom_call" | custom-call | tf_op jit(solution)/shard_map/pallas_call | solution.py:58
  55.5 0.4 fusion.8
  55.9 1.3 convolution_multiply_fusion.2
  57.2 1.4 fusion.16
  58.6 32.1 %shard_map.111 = (bf16[4,64,1024]{2,1,0:T(8,128)(2,1)S(1)}, bf16[4,256,2048]{2,1,0:T(8,128)(2,1)S(1)}, bf16[4,256,256]{2,1,0:T(8,128)(2,1)S(1)}, f32[4,1,2048]{2,1,0:T(1,128)S(1)}) custom-call(bf16[4,64,1024]{2,1,0:T(8,128)(2,1)S(1)} %bitcast.57, bf16[256,2048]{1,0:T(8,128)(2,1)S(1)} %get-tuple-element.29.block, bf16[256,1024]{1,0:T(8,128)(2,1)S(1)} %bitcast.56, ...), custom_call_target="tpu_custom_call" | custom-call | tf_op jit(solution)/shard_map/pallas_call | solution.py:166
  90.7 0.0 copy-start
  90.7 2.0 %copy-done = bf16[4,256,2048]{2,1,0:T(8,128)(2,1)} copy-done((bf16[4,256,2048]{2,1,0:T(8,128)(2,1)}, bf16[4,256,2048]{2,1,0:T(8,128)(2,1)S(1)}, u32[]{:S(2)}) %copy-start) | copy-done | bytes 4194328
  92.7 0.6 reduce_sum.59
  93.3 0.0 copy-start.10
  93.3 4.6 %fusion.7.block = bf16[256,2048]{1,0:T(8,128)(2,1)S(1)} fusion(bf16[256,1024]{1,0:T(8,128)(2,1)S(1)} %bitcast.58, bf16[2048,1024]{1,0:T(8,128)(2,1)} %param.8, f32[256,2048]{1,0:T(8,128)} %get-tuple-element.34), kind=kOutput, calls=%fused_computation.18 | convolution fusion | flops 1078460416 | bytes 7864320 | tf_op jit(solution)/shard_map/dot_general | solution.py:261
  97.9 0.0 copy-done.10
  97.9 0.0 copy-start.1
  97.9 1.3 convolution_convert_fusion
  99.2 0.9 copy-done.1
  100.1 2.6 %convolution_bitcast_fusion.2 = f32[256,2048]{1,0:T(8,128)} fusion(bf16[4,256,2048]{2,1,0:T(8,128)(2,1)S(1)} %copy-done.1, bf16[4,256,256]{2,1,0:T(8,128)(2,1)S(1)} %get-tuple-element.18), kind=kOutput, calls=%fused_computation.12 | convolution fusion | flops 1074528256 | bytes 6815744 | tf_op jit(solution)/shard_map/dot_general | solution.py:258
  102.7 0.0 copy-start.3
  102.7 2.6 %convolution_bitcast_fusion.3 = f32[256,2048]{1,0:T(8,128)} fusion(bf16[4,256,256]{2,1,0:T(8,128)(2,1)S(1)} %get-tuple-element.18, bf16[4,256,2048]{2,1,0:T(8,128)(2,1)S(1)} %copy-done.1), kind=kOutput, calls=%fused_computation.13 | convolution fusion | flops 1073741824 | bytes 6815744 | tf_op jit(solution)/shard_map/dot_general | solution.py:255
  105.3 32.3 %shard_map.112 = (bf16[4,64,1024]{2,1,0:T(8,128)(2,1)S(1)}, bf16[4,256,2048]{2,1,0:T(8,128)(2,1)S(1)}, bf16[4,256,256]{2,1,0:T(8,128)(2,1)S(1)}, f32[4,1,128]{2,1,0:T(1,128)}) custom-call(bf16[4,64,1024]{2,1,0:T(8,128)(2,1)S(1)} %bitcast.60, bf16[256,2048]{1,0:T(8,128)(2,1)S(1)} %fusion.7.block, bf16[256,1024]{1,0:T(8,128)(2,1)S(1)} %bitcast.59, ...), custom_call_target="tpu_custom_call" | custom-call | tf_op jit(solution)/shard_map/pallas_call | solution.py:166
  137.6 0.0 copy-done.3
  137.6 2.2 %fusion.6 = bf16[256,2048]{1,0:T(8,128)(2,1)} fusion(bf16[4,256,256]{2,1,0:T(8,128)(2,1)S(1)} %get-tuple-element.23, bf16[4,256,2048]{2,1,0:T(8,128)(2,1)S(1)} %copy-done.3), kind=kOutput, calls=%fused_computation.17 | convolution fusion | flops 1074266112 | bytes 5767168 | tf_op jit(solution)/shard_map/dot_general | solution.py:271
  139.8 2.2 %fusion.5 = bf16[256,2048]{1,0:T(8,128)(2,1)} fusion(bf16[4,256,256]{2,1,0:T(8,128)(2,1)S(1)} %get-tuple-element.20, bf16[4,256,2048]{2,1,0:T(8,128)(2,1)S(1)} %get-tuple-element.22), kind=kOutput, calls=%fused_computation.16 | convolution fusion | flops 1074266112 | bytes 5767168 | tf_op jit(solution)/shard_map/dot_general | solution.py:268
  142.1 0.8 copy.35
  (6 shorter events, 0.1 us)
Async XLA Ops:
  0.6 5.3 %copy-start.9 = (bf16[1024,2048]{1,0:T(8,128)(2,1)S(1)}, bf16[1024,2048]{1,0:T(8,128)(2,1)}, u32[]{:S(2)}) copy-start(bf16[1024,2048]{1,0:T(8,128)(2,1)} %param.7) | copy-start | bytes 12582916
  0.6 5.3 %copy-start.4 = (bf16[256,1024]{1,0:T(8,128)(2,1)S(1)}, bf16[256,1024]{1,0:T(8,128)(2,1)}, u32[]{:S(2)}) copy-start(bf16[256,1024]{1,0:T(8,128)(2,1)} %wide.1) | copy-start | bytes 1572868
  0.7 5.3 %copy-start.7 = (f32[2048]{0:T(1024)S(1)}, f32[2048]{0:T(1024)}, u32[]{:S(2)}) copy-start(f32[2048]{0:T(1024)} %param.11) | copy-start | bytes 24580
  6.0 2.7 %copy-start.8 = (bf16[2048,1024]{1,0:T(8,128)(2,1)S(1)}, bf16[2048,1024]{1,0:T(8,128)(2,1)}, u32[]{:S(2)}) copy-start(bf16[2048,1024]{1,0:T(8,128)(2,1)} %param.8) | copy-start | bytes 12582916
  8.7 38.9 %copy-start.5 = (bf16[2048,1024]{1,0:T(8,128)(2,1)S(1)}, bf16[2048,1024]{1,0:T(8,128)(2,1)}, u32[]{:S(2)}) copy-start(bf16[2048,1024]{1,0:T(8,128)(2,1)} %param.10) | copy-start | bytes 12582916
  10.0 38.9 %copy-start.6 = (bf16[2048,1024]{1,0:T(8,128)(2,1)S(1)}, bf16[2048,1024]{1,0:T(8,128)(2,1)}, u32[]{:S(2)}) copy-start(bf16[2048,1024]{1,0:T(8,128)(2,1)} %param.9) | copy-start | bytes 12582916
  45.6 1.9 %copy-start.2 = (bf16[4,256,2048]{2,1,0:T(8,128)(2,1)}, bf16[4,256,2048]{2,1,0:T(8,128)(2,1)S(1)}, u32[]{:S(2)}) copy-start(bf16[4,256,2048]{2,1,0:T(8,128)(2,1)S(1)} %get-tuple-element.24) | copy-start | bytes 12582916
  90.7 2.0 %copy-start = (bf16[4,256,2048]{2,1,0:T(8,128)(2,1)}, bf16[4,256,2048]{2,1,0:T(8,128)(2,1)S(1)}, u32[]{:S(2)}) copy-start(bf16[4,256,2048]{2,1,0:T(8,128)(2,1)S(1)} %get-tuple-element.19) | copy-start | bytes 12582916
  93.3 4.6 %copy-start.10 = (bf16[1024,2048]{1,0:T(8,128)(2,1)S(1)}, bf16[1024,2048]{1,0:T(8,128)(2,1)}, u32[]{:S(2)}) copy-start(bf16[1024,2048]{1,0:T(8,128)(2,1)} %param.7) | copy-start | bytes 12582916
  97.9 2.2 %copy-start.1 = (bf16[4,256,2048]{2,1,0:T(8,128)(2,1)S(1)}, bf16[4,256,2048]{2,1,0:T(8,128)(2,1)}, u32[]{:S(2)}) copy-start(bf16[4,256,2048]{2,1,0:T(8,128)(2,1)} %copy-done) | copy-start | bytes 12582916
  102.7 34.9 %copy-start.3 = (bf16[4,256,2048]{2,1,0:T(8,128)(2,1)S(1)}, bf16[4,256,2048]{2,1,0:T(8,128)(2,1)}, u32[]{:S(2)}) copy-start(bf16[4,256,2048]{2,1,0:T(8,128)(2,1)} %copy-done.2) | copy-start | bytes 12582916
